TPU v7x, 32 devices: a whole 2x2x4 slice. The times are simulated.
32 devices in a mesh: ctx: 16 (over z, y, x), tp: 2 (over core).
Axes of the slice: x: 2, y: 2, z: 4, core: 2. Of those that a mesh axis runs over, the one named last changes fastest.
Arguments:
- tokens: bfloat16 [8192, 5120], P('ctx', 'tp'), may hold values from -6 to 6
- norm_gain: float32 [5120], replicated, may hold values from 0.1 to 1.9
- w_query: bfloat16 [5120, 5120], P('ctx', 'tp'), may hold values from -0.078125 to 0.078125
- cache_keys: bfloat16 [8192, 1024], P('ctx', 'tp'), may hold values from -100 to 100
- cache_values: bfloat16 [8192, 1024], P('ctx', 'tp'), may hold values from -6 to 6
- doc_start: int32 [8192], P('ctx'), may hold values from 0 to 8191, as said below
- tile_mask: int32 [64, 64], P('ctx'), may hold values from 0 to 1, as said below
Outputs:
- attended: bfloat16 [8192, 5120], P('ctx', 'tp')
Inputs may be any that keep to these rules, and one draw needn't show every extreme that they name: Documents are contiguous: doc_start is the same within a document and i - 2048 < doc_start[i] <= i; some document has exactly 2048 tokens. `tile_mask`: every diagonal tile is 1.
All inputs are finite; a program needn't handle non-finite values.
Results may differ from a plain program's by a relative error of at most 0.012.
The roundings to bfloat16 on the way count: a program that leaves them out, or rounds other values in their place, can miss the bound.
Values may be sent and summed in bfloat16 or wider, within the bound.
No kernel may reach another device: no remote copies, remote signals or barrier semaphores. Data moves between devices by JAX's collectives and lax.ppermute only.
A program may use at most 256 MiB of HBM per device.

v0:
```python
import math

import jax
import jax.numpy as jnp
from jax import lax
from jax.experimental import pallas as pl
from jax.experimental.pallas import tpu as pltpu
from jax.sharding import PartitionSpec as P

HD = 128
TILE = 128
MAXDOC = 2048
KEYS = 512
QUERIES = 256
CHUNKS = 4
FAR = 1 << 30
MASKED = -1e30


epsilon = 1e-05
exp2_scale = math.log2(math.e) / HD**0.5


def rows_kernel(counts, distances, shapes, info, marks_smem, marks_ref, *refs):
    parts, kv_count, mask_width = counts
    tok_rows, shard_rows, source_rows = shapes
    n = len(distances)
    token_hbm = [refs[k * parts : (k + 1) * parts] for k in range(n)]
    w_hbm = refs[n * parts]
    kv_hbm = refs[n * parts + 1 :][:kv_count]
    out_hbm = refs[n * parts + 1 + kv_count :][:n]
    scratch = refs[n * parts + 1 + kv_count + n :]
    token_ref, w_ref, key_ref, value_ref, total_ref, query_ref, doc_full, acc_ref, max_ref, sum_ref, out_ref = scratch[:11]
    token_sem, w_sem, kv_sem, out_sem = scratch[11:]
    columns = w_ref.shape[1]
    heads = columns // HD
    depth = w_ref.shape[0]
    blocks = depth // source_rows
    halves = kv_hbm[0].shape[0]
    swap = info[1]
    chunk = depth // CHUNKS
    chunks_part = CHUNKS // parts
    doc_rows = tok_rows // TILE
    window_rows = halves * kv_count * shard_rows
    base = window_rows - kv_count * shard_rows

    def token_copy(ref, at, c, slot):
        return pltpu.make_async_copy(
            ref.at[:, at * chunk : (at + 1) * chunk],
            token_ref.at[slot, :, c * chunk : (c + 1) * chunk],
            token_sem.at[slot, c],
        )

    def fetch_tokens(k, c):
        token_copy(token_hbm[k][c // chunks_part], c % chunks_part, c, k % 2).start()

    def rows_of(c):
        return lax.bitwise_xor(info[2], c // chunks_part) * chunks_part + c % chunks_part

    def w_copy(at, place):
        target = pl.ds(pl.multiple_of(place * source_rows, 16), source_rows)
        return pltpu.make_async_copy(w_hbm.at[at], w_ref.at[target], w_sem.at[place])

    blocks_chunk = blocks // CHUNKS

    def kv_copy(ref, half, which, place):
        target = pl.ds(pl.multiple_of(KEYS + place * shard_rows, 16), shard_rows)
        return pltpu.make_async_copy(
            ref.at[half, which], (key_ref, value_ref)[which].at[target], kv_sem.at[place, which]
        )

    def out_copy(k, slot):
        return pltpu.make_async_copy(out_ref.at[slot], out_hbm[k], out_sem.at[slot])

    for c in range(CHUNKS):
        fetch_tokens(0, c)
        for at in range(blocks_chunk):
            place = rows_of(c) * blocks_chunk + at
            w_copy(lax.bitwise_xor(swap, place), place).start()
    for at in range(kv_count):
        for half in range(halves):
            for which in range(2):
                kv_copy(kv_hbm[at], half, which, half * kv_count + lax.bitwise_xor(swap, at)).start()
    key_ref[0:KEYS, :] = jnp.zeros((KEYS, HD), jnp.bfloat16)
    value_ref[0:KEYS, :] = jnp.zeros((KEYS, HD), jnp.bfloat16)

    stacked = heads * QUERIES
    subs = QUERIES // TILE

    def one_rows(k, carry):
        slot = lax.rem(k, 2)
        for ahead in range(1, n):

            @pl.when(k == ahead - 1)
            def _():
                for c in range(CHUNKS):
                    fetch_tokens(ahead, c)

        for c in range(CHUNKS):
            token_copy(token_hbm[0][0], 0, c, slot).wait()

            @pl.when(k == 0)
            def _():
                for at in range(blocks_chunk):
                    w_copy(0, rows_of(c) * blocks_chunk + at).wait()

            for first in range(0, tok_rows, QUERIES):
                piece = jnp.dot(
                    token_ref[slot, first : first + QUERIES, c * chunk : (c + 1) * chunk],
                    w_ref[pl.ds(pl.multiple_of(rows_of(c) * chunk, 16), chunk), :],
                    preferred_element_type=jnp.float32,
                )
                if c == 0:
                    total_ref[first : first + QUERIES, :] = piece
                else:
                    total_ref[first : first + QUERIES, :] += piece
        for tile in range(tok_rows // QUERIES):
            for head in range(heads):
                at = (tile * heads + head) * QUERIES
                query_ref[at : at + QUERIES, :] = total_ref[
                    tile * QUERIES : (tile + 1) * QUERIES, head * HD : (head + 1) * HD
                ].astype(jnp.bfloat16)

        @pl.when(k == 0)
        def _():
            for place in range(kv_count * halves):
                for which in range(2):
                    kv_copy(kv_hbm[0], 0, which, place).wait()

        @pl.when(k >= 2)
        def _():
            out_copy(0, slot).wait()

        distance = jnp.int32(distances[0])
        for other in range(1, n):
            distance = jnp.where(k == other, distances[other], distance)
        rows_first = base + lax.bitwise_xor(swap, distance) * tok_rows

        def one_tile(tile, carry):
            query = query_ref[pl.ds(pl.multiple_of(tile * stacked, stacked), stacked), :]
            row_first = rows_first + tile * QUERIES
            end = row_first + QUERIES
            for sub in range(subs):
                docs_row = marks_ref[k, pl.ds(tile * subs + sub, 1), :].astype(jnp.float32)
                doc_full[sub] = jnp.transpose(jnp.broadcast_to(docs_row, (TILE, TILE))).astype(jnp.int32)
            first_key = marks_smem[k, tile * subs, 0] - info[0]
            count = (end - first_key + KEYS - 1) // KEYS

            def one_block(back, carry):
                start = end - (back + 1) * KEYS
                at = pl.multiple_of(start + KEYS, TILE)
                keys = key_ref[pl.ds(at, KEYS), :]
                values = value_ref[pl.ds(at, KEYS), :]
                scores = lax.dot_general(query, keys, (((1,), (1,)), ((), ())), preferred_element_type=jnp.float32)
                key_tile = (info[0] + start) // TILE
                lane = lax.broadcasted_iota(jnp.int32, (TILE, TILE), 1)
                row = lax.broadcasted_iota(jnp.int32, (TILE, TILE), 0)
                masks = []
                for sub in range(subs):
                    causal = row + (row_first + sub * TILE - start)
                    docs = doc_full[sub] - (info[0] + start)
                    pieces = []
                    for m in range(KEYS // TILE):
                        column = lax.min(lax.max(key_tile + m, 0), mask_width - 1)
                        flat = (tile * subs + sub) * mask_width + column
                        shut = jnp.where(marks_smem[k, doc_rows + flat // TILE, lax.rem(flat, TILE)] == 1, 0, FAR)
                        pieces.append((lane <= causal - m * TILE) & (lane >= docs + (shut - m * TILE)))
                    masks.append(jnp.concatenate(pieces, axis=1))
                visible = jnp.concatenate(masks, axis=0)
                scores = jnp.where(visible[None], scores.reshape(heads, QUERIES, KEYS), MASKED).reshape(stacked, KEYS)
                old = max_ref[...]
                new = jnp.maximum(old, jnp.max(scores, axis=1, keepdims=True))
                alpha = jnp.exp2((old - new) * exp2_scale)
                shift = jnp.concatenate([new * exp2_scale] * (KEYS // HD), axis=1)
                weights = jnp.exp2(scores * exp2_scale - shift)
                max_ref[...] = new
                folded = weights[:, :HD]
                for m in range(1, KEYS // HD):
                    folded = folded + weights[:, m * HD : (m + 1) * HD]
                sum_ref[...] = sum_ref[...] * alpha + folded
                product = jnp.dot(weights.astype(jnp.bfloat16), values, preferred_element_type=jnp.float32)
                acc_ref[...] = acc_ref[...] * alpha + product
                return carry

            max_ref[...] = jnp.full(max_ref.shape, MASKED, jnp.float32)
            sum_ref[...] = jnp.zeros(sum_ref.shape, jnp.float32)
            acc_ref[...] = jnp.zeros(acc_ref.shape, jnp.float32)
            lax.fori_loop(0, count, one_block, 0)
            result = acc_ref[...] / jnp.sum(sum_ref[...], axis=1, keepdims=True)
            for head in range(heads):
                out_ref[slot, pl.ds(pl.multiple_of(tile * QUERIES, QUERIES), QUERIES), head * HD : (head + 1) * HD] = (
                    result[head * QUERIES : (head + 1) * QUERIES].astype(out_ref.dtype)
                )
            return carry

        lax.fori_loop(0, tok_rows // QUERIES, one_tile, 0)
        for at in range(n):

            @pl.when(k == at)
            def _():
                out_copy(at, at % 2).start()

        return carry

    lax.fori_loop(0, n, one_rows, 0)
    for k in range(max(n - 2, 0), n):
        out_copy(k, k % 2).wait()


def attend(info, marks, distances, token_parts, w_blocks, kv_parts, mask_width):
    n = len(distances)
    parts = len(token_parts[0])
    rows = token_parts[0][0].shape[0]
    source_rows, columns = w_blocks.shape[1:]
    depth = w_blocks.shape[0] * source_rows
    heads = columns // HD
    shard_rows = kv_parts[0].shape[2]
    shards = len(kv_parts) * kv_parts[0].shape[0]
    vmem = pl.BlockSpec(memory_space=pltpu.VMEM)
    smem = pl.BlockSpec(memory_space=pltpu.SMEM)
    leave = pl.BlockSpec(memory_space=pl.ANY)
    arrays = [part for block in token_parts for part in block] + [w_blocks] + list(kv_parts)
    counts = (parts, len(kv_parts), mask_width)
    tile_rows = heads * QUERIES

    def kernel(*refs):
        rows_kernel(counts, distances, (rows, shard_rows, source_rows), *refs)

    return pl.pallas_call(
        kernel,
        out_shape=[jax.ShapeDtypeStruct((rows, columns), jnp.bfloat16)] * n,
        in_specs=[smem, smem, vmem] + [leave] * len(arrays),
        out_specs=[leave] * n,
        scratch_shapes=[
            pltpu.VMEM((2, rows, depth), jnp.bfloat16),
            pltpu.VMEM((depth, columns), jnp.bfloat16),
            pltpu.VMEM((KEYS + shards * shard_rows, HD), jnp.bfloat16),
            pltpu.VMEM((KEYS + shards * shard_rows, HD), jnp.bfloat16),
            pltpu.VMEM((rows, columns), jnp.float32),
            pltpu.VMEM((rows * heads, HD), jnp.bfloat16),
            pltpu.VMEM((QUERIES // TILE, TILE, TILE), jnp.int32),
            pltpu.VMEM((tile_rows, HD), jnp.float32),
            pltpu.VMEM((tile_rows, HD), jnp.float32),
            pltpu.VMEM((tile_rows, HD), jnp.float32),
            pltpu.VMEM((2, rows, columns), jnp.bfloat16),
            pltpu.SemaphoreType.DMA((2, CHUNKS)),
            pltpu.SemaphoreType.DMA((w_blocks.shape[0],)),
            pltpu.SemaphoreType.DMA((shards, 2)),
            pltpu.SemaphoreType.DMA((2,)),
        ],
        compiler_params=pltpu.CompilerParams(vmem_limit_bytes=60 << 20),
        cost_estimate=pl.CostEstimate(
            flops=n * (2 * rows * depth * columns + 4 * rows * columns * 1024),
            bytes_accessed=2 * (n * rows * depth + depth * columns + shards * 2 * shard_rows * HD + n * rows * columns),
            transcendentals=n * rows * heads * 1024,
        ),
    )(info, marks, marks, *arrays)


def marks_of(doc_start, tile_mask):
    return jnp.concatenate([doc_start.reshape(-1, TILE), tile_mask.reshape(-1, TILE)])


def planar(tokens, norm_gain, w_query, cache_keys, cache_values, doc_start, tile_mask, group):
    devices = lax.axis_size("ctx")
    index = lax.axis_index("ctx")
    core = lax.axis_index("tp")
    place = lax.rem(index, group)
    tok_rows, width = tokens.shape
    kv_width = cache_keys.shape[1] // group
    q_width = w_query.shape[1] // group
    rows = group * tok_rows
    lines = [[first + k for first in range(0, devices, group)] for k in range(group)]
    far = range(1, group)

    def swapped(block, distance):
        return lax.ppermute(block, "ctx", [(i, i ^ distance) for i in range(devices)])

    def other_core(block):
        return lax.ppermute(block, "tp", [(0, 1), (1, 0)])

    def columns_for(array, distance, first, size, of, axis):
        at = lax.bitwise_xor(place, distance) * of + first
        return lax.dynamic_slice_in_dim(array, at, size, axis)

    def after(values, *earlier):
        flat = lax.optimization_barrier((tuple(values), tuple(earlier)))
        return list(flat[0])

    first_columns = (q_width // HD + 1) // 2 * HD
    cuts = ((0, first_columns), (first_columns, q_width))

    marks_own = marks_of(doc_start, tile_mask)
    w_first = [columns_for(w_query, d, cuts[0][0], cuts[0][1] - cuts[0][0], q_width, 1) for d in range(group)]
    w_first = w_first[:1] + [swapped(w_first[d], d) for d in far]
    hop = [(i, i + group) for i in range(devices - group)]
    kv_before = [lax.ppermute(array, "ctx", hop) for array in (cache_keys, cache_values)]
    (marks_sent,) = after([marks_own], *w_first)
    marks = [marks_own] + [swapped(marks_sent, d) for d in far]

    float_tokens = tokens.astype(jnp.float32)
    squares = jnp.sum(float_tokens * float_tokens, axis=-1)
    squares = squares + other_core(squares)
    inverse = lax.rsqrt(squares / (2 * width) + epsilon)
    gain = lax.dynamic_slice_in_dim(norm_gain, core * width, width, 0)
    normed = (float_tokens * inverse[:, None] * gain).astype(jnp.bfloat16)

    w_first = after(w_first, *kv_before)
    w_chunks = [lax.all_gather(jnp.stack(w_first), "ctx", axis=0, tiled=True, axis_index_groups=lines)]

    def kv_for(d):
        arrays = (*kv_before, cache_keys, cache_values)
        return jnp.stack([columns_for(array, d, 0, kv_width, kv_width, 1) for array in arrays]).reshape(
            2, 2, tok_rows, kv_width
        )

    w_second = [columns_for(w_query, d, cuts[1][0], cuts[1][1] - cuts[1][0], q_width, 1) for d in range(group)]
    (normed,) = after([normed], *marks)
    w_second = after(w_second, *marks)
    from_x, from_y = swapped(normed, 1), swapped(normed, 2)
    w_second = w_second[:1] + [swapped(w_second[d], d) for d in far]
    mine_other = other_core(normed)
    kv_cut = [kv_for(d) for d in range(group)]
    kv_parts = kv_cut[:1] + [swapped(kv_cut[d], d) for d in far]
    (w_after,) = after([jnp.stack(w_second)], *kv_parts)
    w_chunks.append(lax.all_gather(w_after, "ctx", axis=0, tiled=True, axis_index_groups=lines))

    half = width // 2
    from_x, from_y = after([from_x, from_y], w_after)
    corner_a, corner_b = swapped(from_y[:, :half], 1), swapped(from_x[:, half:], 2)
    token_parts = [[normed, mine_other]] + [[from_x, other_core(from_x)], [from_y, other_core(from_y)]]

    info = jnp.stack([(index // group - 1) * rows, place, core]).astype(jnp.int32)
    width_mask = tile_mask.shape[1]

    def call(distances, chunk, *earlier):
        chosen = [token_parts[d] for d in distances]
        (start,) = after([info], *earlier)
        picked = jnp.stack([marks[d] for d in distances])
        return attend(start, picked, distances, chosen, chunk, kv_parts, width_mask)

    pieces, last = {}, ()
    for chunk, distances in ((0, (2, 1, 0)), (0, (3,)), (1, (3, 2, 1)), (1, (0,))):
        if distances == (3,):
            corner = jnp.concatenate(after([corner_a, corner_b], *last), axis=1)
            token_parts.append([corner, other_core(corner)])
        outs = call(distances, w_chunks[chunk], *last)
        last = outs[:1]
        pieces.update({(d, chunk): swapped(out, d) if d else out for d, out in zip(distances, outs)})
    return joined(info, pieces, q_width, [low for low, _ in cuts], group * q_width)


def joined(info, pieces, q_width, lows, columns):
    keys = sorted(pieces)
    rows = pieces[keys[0]].shape[0]
    vmem = pl.BlockSpec(memory_space=pltpu.VMEM)

    def kernel(info_ref, *refs):
        out_ref = refs[-1]
        for k, (distance, chunk) in enumerate(keys):
            at = pl.multiple_of(lax.bitwise_xor(info_ref[1], distance) * q_width + lows[chunk], HD)
            out_ref[:, pl.ds(at, refs[k].shape[1])] = refs[k][...]

    return pl.pallas_call(
        kernel,
        out_shape=jax.ShapeDtypeStruct((rows, columns), jnp.bfloat16),
        in_specs=[pl.BlockSpec(memory_space=pltpu.SMEM)] + [vmem] * len(keys),
        out_specs=vmem,
        cost_estimate=pl.CostEstimate(flops=0, bytes_accessed=4 * rows * columns, transcendentals=0),
    )(info, *[pieces[key] for key in keys])


def plain(tokens, norm_gain, w_query, cache_keys, cache_values, doc_start, tile_mask):
    devices = lax.axis_size("ctx")
    index = lax.axis_index("ctx")
    tok_rows = tokens.shape[0]
    float_tokens = lax.all_gather(tokens, "tp", axis=1, tiled=True).astype(jnp.float32)
    inverse = lax.rsqrt(jnp.mean(float_tokens * float_tokens, axis=-1, keepdims=True) + epsilon)
    normed = (float_tokens * inverse * norm_gain).astype(jnp.bfloat16)
    kv_heads = cache_keys.shape[1] // HD
    q_width = w_query.shape[1] // kv_heads
    w_blocks = lax.all_gather(w_query, "ctx", axis=0)
    reach = (MAXDOC + tok_rows - 2) // tok_rows
    kv_own = jnp.stack([cache_keys, cache_values])
    shards = [
        lax.ppermute(kv_own, "ctx", [(i, i + distance) for i in range(devices - distance)])
        for distance in range(reach, 0, -1)
    ]
    kv_window = jnp.stack(shards + [kv_own])
    info = jnp.stack([(index - reach) * tok_rows, jnp.int32(0), jnp.int32(0)]).astype(jnp.int32)
    marks = marks_of(doc_start, tile_mask)[None]
    outs = [
        attend(
            info,
            marks,
            (0,),
            [[normed]],
            w_blocks[:, :, head * q_width : (head + 1) * q_width],
            [kv_window[:, :, :, head * HD : (head + 1) * HD]],
            tile_mask.shape[1],
        )[0]
        for head in range(kv_heads)
    ]
    return outs[0] if kv_heads == 1 else jnp.concatenate(outs, axis=1)


def on_device(*arrays):
    kv_heads = arrays[3].shape[1] // HD
    group = 4
    rows = group * arrays[0].shape[0]
    if kv_heads == group and lax.axis_size("ctx") % group == 0 and lax.axis_size("tp") == 2 and rows >= MAXDOC - 1:
        return planar(*arrays, group)
    return plain(*arrays)


def solution(mesh):
    return jax.shard_map(
        on_device,
        mesh=mesh,
        in_specs=(
            P("ctx", "tp"),
            P(),
            P("ctx", "tp"),
            P("ctx", "tp"),
            P("ctx", "tp"),
            P("ctx"),
            P("ctx", None),
        ),
        out_specs=P("ctx", "tp"),
        check_vma=False,
    )
```

profile of v0, /device:TPU:10, one launch (start us, length us, event | category | flops | bytes accessed | tf_op | source)
XLA Modules:
  0.0 247.7 jit_solution(57638285457264489)
XLA Ops:
  6.5 3.6 %collective-permute-start.12 = (bf16[512,512]{1,0:T(8,128)(2,1)}, bf16[512,512]{1,0:T(8,128)(2,1)}, u32[]{:S(2)}, u32[]{:S(2)}) collective-permute-start(bf16[512,512]{1,0:T(8,128)(2,1)} %param.10), channel_id=1, source_target_pairs={{0,8},{2,10},{4,12},{6,14},{8,16},{10,18},{12,20},{14,22},{16,24},... | collective-permute-start | bytes 1572872 | tf_op jit(solution)/shard_map/ppermute | solution.py:297
  10.2 3.5 %collective-permute-start.13 = (bf16[512,512]{1,0:T(8,128)(2,1)}, bf16[512,512]{1,0:T(8,128)(2,1)S(1)}, u32[]{:S(2)}, u32[]{:S(2)}) collective-permute-start(bf16[512,512]{1,0:T(8,128)(2,1)} %param.11), channel_id=1, source_target_pairs={{0,8},{2,10},{4,12},{6,14},{8,16},{10,18},{12,20},{14,22},{16,24},... | collective-permute-start | bytes 1572872 | tf_op jit(solution)/shard_map/ppermute | solution.py:297
  13.7 2.3 fusion
  16.1 2.3 constant_dynamic-slice_fusion.4
  19.0 1.5 collective-permute-start.1
  20.6 1.4 collective-permute-start.2
  22.2 5.4 %collective-permute-done = bf16[320,384]{1,0:T(8,128)(2,1)} collective-permute-done((bf16[320,384]{1,0:T(8,128)(2,1)}, bf16[320,384]{1,0:T(8,128)(2,1)}, u32[]{:S(2)}, u32[]{:S(2)}) %collective-permute-start) | collective-permute-done | bytes 245792 | tf_op jit(solution)/shard_map/ppermute | solution.py:277
  27.6 4.0 %collective-permute-done.1 = bf16[320,384]{1,0:T(8,128)(2,1)} collective-permute-done((bf16[320,384]{1,0:T(8,128)(2,1)}, bf16[320,384]{1,0:T(8,128)(2,1)}, u32[]{:S(2)}, u32[]{:S(2)}) %collective-permute-start.1) | collective-permute-done | bytes 245792 | tf_op jit(solution)/shard_map/ppermute | solution.py:277
  31.5 1.6 collective-permute-done.2
  34.0 1.5 collective-permute-start.4
  36.7 2.5 %pad_maximum_fusion = bf16[4,320,384]{2,1,0:T(8,128)(2,1)} fusion(bf16[1,320,384]{2,1,0:T(8,128)(2,1)} %bitcast.34, bf16[1,320,384]{2,1,0:T(8,128)(2,1)} %bitcast.33, bf16[1,320,384]{2,1,0:T(8,128)(2,1)} %bitcast.32, bf16[1,320,384]{2,1,0:T(8,128)(2,1)S(1)} %bitcast.57), kind=kLoop, calls=%fused_computation.5 | loop fusion | flops 1474560 | bytes 1966080 | tf_op jit(solution)/shard_map/stack | solution.py:309
  39.3 2.2 fusion.2.refs_7_.refs_3_
  42.3 1.5 collective-permute-start.8
  48.4 1.6 collective-permute-start.10
  53.1 51.6 %collective-permute-done.11 = bf16[320,256]{1,0:T(8,128)(2,1)S(1)} collective-permute-done((bf16[320,256]{1,0:T(8,128)(2,1)S(1)}, bf16[320,256]{1,0:T(8,128)(2,1)S(1)}, u32[]{:S(2)}, u32[]{:S(2)}) %collective-permute-start.11) | collective-permute-done | bytes 163872 | tf_op jit(solution)/shard_map/ppermute | solution.py:277
  104.8 2.0 collective-permute-start.14
  106.8 1.8 collective-permute-done.9
  108.8 2.0 collective-permute-start.16
  112.6 7.1 %collective-permute-done.14.refs_11_.refs_7_ = bf16[2,2,512,128]{3,2,1,0:T(8,128)(2,1)S(1)} collective-permute-done((bf16[2,2,512,128]{3,2,1,0:T(8,128)(2,1)S(1)}, bf16[2,2,512,128]{3,2,1,0:T(8,128)(2,1)S(1)}, u32[]{:S(2)}, u32[]{:S(2)}) %collective-permute-start.14) | collective-permute-done | bytes 524320 | tf_op jit(solution)/shard_map/ppermute | solution.py:277
  119.8 9.6 %collective-permute-done.15.refs_12_.refs_8_ = bf16[2,2,512,128]{3,2,1,0:T(8,128)(2,1)} collective-permute-done((bf16[2,2,512,128]{3,2,1,0:T(8,128)(2,1)}, bf16[2,2,512,128]{3,2,1,0:T(8,128)(2,1)}, u32[]{:S(2)}, u32[]{:S(2)}) %collective-permute-start.15) | collective-permute-done | bytes 524320 | tf_op jit(solution)/shard_map/ppermute | solution.py:277
  130.0 2.5 %slice.6 = bf16[512,1280]{1,0:T(8,128)(2,1)} slice(bf16[512,2560]{1,0:T(8,128)(2,1)} %collective-permute-done.8.refs_3_.refs_5_), slice={[0:512], [0:1280]} | slice | bytes 2621440 | tf_op jit(solution)/shard_map/slice | solution.py:330
  132.5 2.5 slice.7
  139.9 34.1 %shard_map.73 = (bf16[512,384]{1,0:T(8,128)(2,1)}, bf16[512,384]{1,0:T(8,128)(2,1)}, bf16[512,384]{1,0:T(8,128)(2,1)}) custom-call(s32[3]{0:T(128)} %pad_add_fusion.3.refs_0_.info_ref, s32[3,6,128]{2,1,0:T(8,128)} %get-tuple-element.78.refs_1_.refs_2_, s32[3,6,128]{2,1,0:T(8,128)} %get-tuple-element.78.refs_1_.refs_2_, ...), custom_call_target="tpu_custom_call" | custom-call | flops 8455716864 | bytes 22937600 | tf_op jit(solution)/shard_map/pallas_call | solution.py:229
  174.0 1.5 constant_dynamic-update-slice_fusion.1
  175.5 1.4 constant_dynamic-update-slice_fusion.refs_3_
  178.1 3.9 %collective-permute-done.22.refs_4_ = bf16[512,2560]{1,0:T(8,128)(2,1)} collective-permute-done((bf16[512,2560]{1,0:T(8,128)(2,1)S(1)}, bf16[512,2560]{1,0:T(8,128)(2,1)}, u32[]{:S(2)}, u32[]{:S(2)}) %collective-permute-start.22) | collective-permute-done | bytes 2621472 | tf_op jit(solution)/shard_map/ppermute | solution.py:280
  182.0 11.5 %shard_map.74 = bf16[512,384]{1,0:T(8,128)(2,1)} custom-call(s32[3]{0:T(128)} %pad_add_fusion.3.refs_0_.info_ref, s32[1,6,128]{2,1,0:T(8,128)} %bitcast.64, s32[1,6,128]{2,1,0:T(8,128)} %bitcast.65, bf16[512,2560]{1,0:T(8,128)(2,1)} %copy-done.1, bf16[512,2560]{1,0:T(8,128)(2,1)} %collective-permute-done.22.refs_4_, ...), custom_call_target="tpu_custom_call" | custom-call | flops 2818572288 | bytes 11665408 | tf_op jit(solution)/shard_map/pallas_call | solution.py:229
  193.5 3.8 %collective-permute-start.27 = (bf16[512,384]{1,0:T(8,128)(2,1)}, bf16[512,384]{1,0:T(8,128)(2,1)S(1)}, u32[]{:S(2)}, u32[]{:S(2)}) collective-permute-start(bf16[512,384]{1,0:T(8,128)(2,1)} %shard_map.74), channel_id=1, source_target_pairs={{0,6},{2,4},{4,2},{6,0},{8,14},{10,12},{12,10},{14,8},{16,22},{18,... | collective-permute-start | bytes 1179656 | tf_op jit(solution)/shard_map/ppermute | solution.py:277
  197.4 20.9 %shard_map.75 = (bf16[512,256]{1,0:T(8,128)(2,1)}, bf16[512,256]{1,0:T(8,128)(2,1)}, bf16[512,256]{1,0:T(8,128)(2,1)}) custom-call(s32[3]{0:T(128)} %pad_add_fusion.3.refs_0_.info_ref, s32[3,6,128]{2,1,0:T(8,128)} %get-tuple-element.77.refs_1_.refs_2_, s32[3,6,128]{2,1,0:T(8,128)} %get-tuple-element.77.refs_1_.refs_2_, bf16[512,2560]{1,0:T(8,128)(2,1)} %copy-done.1, ...), custom_call_target="tpu_custom_call" | custom-call | flops 5637144576 | bytes 21233664 | tf_op jit(solution)/shard_map/pallas_call | solution.py:229
  219.0 4.2 %collective-permute-start.26 = (bf16[512,256]{1,0:T(8,128)(2,1)}, bf16[512,256]{1,0:T(8,128)(2,1)S(1)}, u32[]{:S(2)}, u32[]{:S(2)}) collective-permute-start(bf16[512,256]{1,0:T(8,128)(2,1)} %get-tuple-element.52), channel_id=1, source_target_pairs={{0,4},{2,6},{4,0},{6,2},{8,12},{10,14},{12,8},{14,10},{16,20},{18,... | collective-permute-start | bytes 786440 | tf_op jit(solution)/shard_map/ppermute | solution.py:277
  223.2 13.2 %shard_map.76.refs_1_ = bf16[512,256]{1,0:T(8,128)(2,1)} custom-call(s32[3]{0:T(128)} %pad_add_fusion.3.refs_0_.info_ref, s32[1,6,128]{2,1,0:T(8,128)} %copy-done.13, s32[1,6,128]{2,1,0:T(8,128)} %copy-done.13, bf16[512,2560]{1,0:T(8,128)(2,1)} %fusion.2.refs_7_.refs_3_, bf16[512,2560]{1,0:T(8,128)(2,1)} %copy-done.2, ...), custom_call_target="tpu_custom_call" | custom-call | flops 1879048192 | bytes 10223616 | tf_op jit(solution)/shard_map/pallas_call | solution.py:229
  237.5 3.4 %shard_map.77 = bf16[512,2560]{1,0:T(8,128)(2,1)} custom-call(s32[3]{0:T(128)} %pad_add_fusion.3.refs_0_.info_ref, bf16[512,384]{1,0:T(8,128)(2,1)} %get-tuple-element.42.refs_0_, bf16[512,256]{1,0:T(8,128)(2,1)} %shard_map.76.refs_1_, bf16[512,384]{1,0:T(8,128)(2,1)} %copy-done.8, bf16[512,256]{1,0:T(8,128)(2,1)} %copy-done.10, bf16[512,384]{1,0:T(8,128)(2,1)} %copy-done.7, ...), custom_call_target="tpu_custom_call" | custom-call | bytes 5242880 | tf_op jit(solution)/shard_map/pallas_call | solution.py:364
  (98 shorter events, 22.0 us)
Async XLA Ops:
  6.5 131.9 %all-gather.3.cloned.1.call-start = ((), (), s32[]{:S(2)}) async-start(), calls=%async_computation | async-start | bytes 4915200 | tf_op jit(solution)/shard_map/all_gather | solution.py:309
  6.5 30.1 %collective-permute-start.12 = (bf16[512,512]{1,0:T(8,128)(2,1)}, bf16[512,512]{1,0:T(8,128)(2,1)}, u32[]{:S(2)}, u32[]{:S(2)}) collective-permute-start(bf16[512,512]{1,0:T(8,128)(2,1)} %param.10), channel_id=1, source_target_pairs={{0,8},{2,10},{4,12},{6,14},{8,16},{10,18},{12,20},{14,22},{16,24},... | collective-permute-start | bytes 1572872 | tf_op jit(solution)/shard_map/ppermute | solution.py:297
  10.2 26.5 %collective-permute-start.13 = (bf16[512,512]{1,0:T(8,128)(2,1)}, bf16[512,512]{1,0:T(8,128)(2,1)S(1)}, u32[]{:S(2)}, u32[]{:S(2)}) collective-permute-start(bf16[512,512]{1,0:T(8,128)(2,1)} %param.11), channel_id=1, source_target_pairs={{0,8},{2,10},{4,12},{6,14},{8,16},{10,18},{12,20},{14,22},{16,24},... | collective-permute-start | bytes 1572872 | tf_op jit(solution)/shard_map/ppermute | solution.py:297
  16.0 4.6 %collective-permute-start.5 = (f32[512]{0:T(512)S(1)}, f32[512]{0:T(512)S(1)}, u32[]{:S(2)}, u32[]{:S(2)}) collective-permute-start(f32[512]{0:T(512)S(1)} %fusion), channel_id=1, source_target_pairs={{0,1},{1,0},{2,3},{3,2},{4,5},{5,4},{6,7},{7,6},{8,9},{9,8},{10,11... | collective-permute-start | bytes 6152 | tf_op jit(solution)/shard_map/ppermute | solution.py:280
  18.5 9.1 %collective-permute-start = (bf16[320,384]{1,0:T(8,128)(2,1)}, bf16[320,384]{1,0:T(8,128)(2,1)}, u32[]{:S(2)}, u32[]{:S(2)}) collective-permute-start(bf16[320,384]{1,0:T(8,128)(2,1)} %get-tuple-element.59), channel_id=1, source_target_pairs={{0,2},{2,0},{4,6},{6,4},{8,10},{10,8},{12,14},{14,12},{16,18},{18,... | collective-permute-start | bytes 737288 | tf_op jit(solution)/shard_map/ppermute | solution.py:277
  19.0 12.5 %collective-permute-start.1 = (bf16[320,384]{1,0:T(8,128)(2,1)}, bf16[320,384]{1,0:T(8,128)(2,1)}, u32[]{:S(2)}, u32[]{:S(2)}) collective-permute-start(bf16[320,384]{1,0:T(8,128)(2,1)} %get-tuple-element.58), channel_id=1, source_target_pairs={{0,4},{2,6},{4,0},{6,2},{8,12},{10,14},{12,8},{14,10},{16,20},{18,... | collective-permute-start | bytes 737288 | tf_op jit(solution)/shard_map/ppermute | solution.py:277
  20.6 12.6 %collective-permute-start.2 = (bf16[320,384]{1,0:T(8,128)(2,1)}, bf16[320,384]{1,0:T(8,128)(2,1)}, u32[]{:S(2)}, u32[]{:S(2)}) collective-permute-start(bf16[320,384]{1,0:T(8,128)(2,1)} %get-tuple-element.57), channel_id=1, source_target_pairs={{0,6},{2,4},{4,2},{6,0},{8,14},{10,12},{12,10},{14,8},{16,22},{18,... | collective-permute-start | bytes 737288 | tf_op jit(solution)/shard_map/ppermute | solution.py:277
  22.1 115.7 %copy-start.13 = (s32[1,6,128]{2,1,0:T(8,128)}, s32[1,6,128]{2,1,0:T(8,128)S(1)}, u32[]{:S(2)}) copy-start(s32[1,6,128]{2,1,0:T(8,128)S(1)} %get-tuple-element.80.refs_1_.refs_2_) | copy-start | bytes 9220
  33.2 8.2 %collective-permute-start.3 = (s32[6,128]{1,0:T(8,128)S(1)}, s32[6,128]{1,0:T(8,128)S(1)}, u32[]{:S(2)}, u32[]{:S(2)}) collective-permute-start(s32[6,128]{1,0:T(8,128)S(1)} %get-tuple-element.29), channel_id=1, source_target_pairs={{0,4},{2,6},{4,0},{6,2},{8,12},{10,14},{12,8},{14,10},{16,20},{18,... | collective-permute-start | bytes 9224 | tf_op jit(solution)/shard_map/ppermute | solution.py:277
  34.0 7.4 %collective-permute-start.4 = (s32[6,128]{1,0:T(8,128)S(1)}, s32[6,128]{1,0:T(8,128)S(1)}, u32[]{:S(2)}, u32[]{:S(2)}) collective-permute-start(s32[6,128]{1,0:T(8,128)S(1)} %get-tuple-element.29), channel_id=1, source_target_pairs={{0,2},{2,0},{4,6},{6,4},{8,10},{10,8},{12,14},{14,12},{16,18},{18,... | collective-permute-start | bytes 9224 | tf_op jit(solution)/shard_map/ppermute | solution.py:277
  35.5 5.9 %collective-permute-start.6 = (s32[6,128]{1,0:T(8,128)S(1)}, s32[6,128]{1,0:T(8,128)S(1)}, u32[]{:S(2)}, u32[]{:S(2)}) collective-permute-start(s32[6,128]{1,0:T(8,128)S(1)} %get-tuple-element.29), channel_id=1, source_target_pairs={{0,6},{2,4},{4,2},{6,0},{8,14},{10,12},{12,10},{14,8},{16,22},{18,... | collective-permute-start | bytes 9224 | tf_op jit(solution)/shard_map/ppermute | solution.py:277
  39.2 158.2 %all-gather.5.cloned.1.call-start = ((), (), s32[]{:S(2)}) async-start(), calls=%async_computation.1 | async-start | bytes 3276800 | tf_op jit(solution)/shard_map/all_gather | solution.py:326
  41.4 88.0 %collective-permute-start.7 = (bf16[512,2560]{1,0:T(8,128)(2,1)}, bf16[512,2560]{1,0:T(8,128)(2,1)}, u32[]{:S(2)}, u32[]{:S(2)}) collective-permute-start(bf16[512,2560]{1,0:T(8,128)(2,1)} %fusion.2.refs_7_.refs_3_), channel_id=1, source_target_pairs={{0,2},{2,0},{4,6},{6,4},{8,10},{10,8},{12,14},{14,12},{16,18},{18,... | collective-permute-start | bytes 7864328 | tf_op jit(solution)/shard_map/ppermute | solution.py:277
  42.3 87.1 %collective-permute-start.8 = (bf16[512,2560]{1,0:T(8,128)(2,1)}, bf16[512,2560]{1,0:T(8,128)(2,1)}, u32[]{:S(2)}, u32[]{:S(2)}) collective-permute-start(bf16[512,2560]{1,0:T(8,128)(2,1)} %fusion.2.refs_7_.refs_3_), channel_id=1, source_target_pairs={{0,4},{2,6},{4,0},{6,2},{8,12},{10,14},{12,8},{14,10},{16,20},{18,... | collective-permute-start | bytes 7864328 | tf_op jit(solution)/shard_map/ppermute | solution.py:277
  46.5 58.3 %collective-permute-start.11 = (bf16[320,256]{1,0:T(8,128)(2,1)S(1)}, bf16[320,256]{1,0:T(8,128)(2,1)S(1)}, u32[]{:S(2)}, u32[]{:S(2)}) collective-permute-start(bf16[320,256]{1,0:T(8,128)(2,1)S(1)} %get-tuple-element.34), channel_id=1, source_target_pairs={{0,6},{2,4},{4,2},{6,0},{8,14},{10,12},{12,10},{14,8},{16,22},{18,... | collective-permute-start | bytes 491528 | tf_op jit(solution)/shard_map/ppermute | solution.py:277
  47.7 60.8 %collective-permute-start.9 = (bf16[320,256]{1,0:T(8,128)(2,1)S(1)}, bf16[320,256]{1,0:T(8,128)(2,1)S(1)}, u32[]{:S(2)}, u32[]{:S(2)}) collective-permute-start(bf16[320,256]{1,0:T(8,128)(2,1)S(1)} %get-tuple-element.32), channel_id=1, source_target_pairs={{0,2},{2,0},{4,6},{6,4},{8,10},{10,8},{12,14},{14,12},{16,18},{18,... | collective-permute-start | bytes 491528 | tf_op jit(solution)/shard_map/ppermute | solution.py:277
  48.4 60.4 %collective-permute-start.10 = (bf16[320,256]{1,0:T(8,128)(2,1)S(1)}, bf16[320,256]{1,0:T(8,128)(2,1)S(1)}, u32[]{:S(2)}, u32[]{:S(2)}) collective-permute-start(bf16[320,256]{1,0:T(8,128)(2,1)S(1)} %get-tuple-element.33), channel_id=1, source_target_pairs={{0,4},{2,6},{4,0},{6,2},{8,12},{10,14},{12,8},{14,10},{16,20},{18,... | collective-permute-start | bytes 491528 | tf_op jit(solution)/shard_map/ppermute | solution.py:277
  104.8 15.0 %collective-permute-start.14 = (bf16[2,2,512,128]{3,2,1,0:T(8,128)(2,1)S(1)}, bf16[2,2,512,128]{3,2,1,0:T(8,128)(2,1)S(1)}, u32[]{:S(2)}, u32[]{:S(2)}) collective-permute-start(bf16[2,2,512,128]{3,2,1,0:T(8,128)(2,1)S(1)} %bitcast.59), channel_id=1, source_target_pairs={{0,2},{2,0},{4,6},{6,4},{8,10},{10,8},{12,14},{14,12},{16,18},{18,... | collective-permute-start | bytes 1572872 | tf_op jit(solution)/shard_map/ppermute | solution.py:277
  108.5 20.9 %collective-permute-start.15 = (bf16[2,2,512,128]{3,2,1,0:T(8,128)(2,1)}, bf16[2,2,512,128]{3,2,1,0:T(8,128)(2,1)}, u32[]{:S(2)}, u32[]{:S(2)}) collective-permute-start(bf16[2,2,512,128]{3,2,1,0:T(8,128)(2,1)} %bitcast.25), channel_id=1, source_target_pairs={{0,4},{2,6},{4,0},{6,2},{8,12},{10,14},{12,8},{14,10},{16,20},{18,... | collective-permute-start | bytes 1572872 | tf_op jit(solution)/shard_map/ppermute | solution.py:277
  108.8 20.6 %collective-permute-start.16 = (bf16[2,2,512,128]{3,2,1,0:T(8,128)(2,1)}, bf16[2,2,512,128]{3,2,1,0:T(8,128)(2,1)}, u32[]{:S(2)}, u32[]{:S(2)}) collective-permute-start(bf16[2,2,512,128]{3,2,1,0:T(8,128)(2,1)} %bitcast.30), channel_id=1, source_target_pairs={{0,6},{2,4},{4,2},{6,0},{8,14},{10,12},{12,10},{14,8},{16,22},{18,... | collective-permute-start | bytes 1572872 | tf_op jit(solution)/shard_map/ppermute | solution.py:277
  119.8 18.6 %collective-permute-start.19 = (bf16[512,2560]{1,0:T(8,128)(2,1)}, bf16[512,2560]{1,0:T(8,128)(2,1)S(1)}, u32[]{:S(2)}, u32[]{:S(2)}) collective-permute-start(bf16[512,2560]{1,0:T(8,128)(2,1)} %fusion.2.refs_7_.refs_3_), channel_id=1, source_target_pairs={{0,1},{1,0},{2,3},{3,2},{4,5},{5,4},{6,7},{7,6},{8,9},{9,8},{10,11... | collective-permute-start | bytes 7864328 | tf_op jit(solution)/shard_map/ppermute | solution.py:280
  129.4 9.0 %collective-permute-start.17 = (bf16[512,2560]{1,0:T(8,128)(2,1)}, bf16[512,2560]{1,0:T(8,128)(2,1)}, u32[]{:S(2)}, u32[]{:S(2)}) collective-permute-start(bf16[512,2560]{1,0:T(8,128)(2,1)} %collective-permute-done.8.refs_3_.refs_5_), channel_id=1, source_target_pairs={{0,1},{1,0},{2,3},{3,2},{4,5},{5,4},{6,7},{7,6},{8,9},{9,8},{10,11... | collective-permute-start | bytes 7864328 | tf_op jit(solution)/shard_map/ppermute | solution.py:280
  129.5 9.0 %collective-permute-start.18 = (bf16[512,2560]{1,0:T(8,128)(2,1)}, bf16[512,2560]{1,0:T(8,128)(2,1)}, u32[]{:S(2)}, u32[]{:S(2)}) collective-permute-start(bf16[512,2560]{1,0:T(8,128)(2,1)} %collective-permute-done.7.refs_5_.refs_7_), channel_id=1, source_target_pairs={{0,1},{1,0},{2,3},{3,2},{4,5},{5,4},{6,7},{7,6},{8,9},{9,8},{10,11... | collective-permute-start | bytes 7864328 | tf_op jit(solution)/shard_map/ppermute | solution.py:280
  134.9 39.0 %collective-permute-start.20 = (bf16[512,1280]{1,0:T(8,128)(2,1)}, bf16[512,1280]{1,0:T(8,128)(2,1)}, u32[]{:S(2)}, u32[]{:S(2)}) collective-permute-start(bf16[512,1280]{1,0:T(8,128)(2,1)} %slice.6), channel_id=1, source_target_pairs={{0,2},{2,0},{4,6},{6,4},{8,10},{10,8},{12,14},{14,12},{16,18},{18,... | collective-permute-start | bytes 3932168 | tf_op jit(solution)/shard_map/ppermute | solution.py:277
  136.0 38.0 %collective-permute-start.21 = (bf16[512,1280]{1,0:T(8,128)(2,1)}, bf16[512,1280]{1,0:T(8,128)(2,1)}, u32[]{:S(2)}, u32[]{:S(2)}) collective-permute-start(bf16[512,1280]{1,0:T(8,128)(2,1)} %slice.7), channel_id=1, source_target_pairs={{0,4},{2,6},{4,0},{6,2},{8,12},{10,14},{12,8},{14,10},{16,20},{18,... | collective-permute-start | bytes 3932168 | tf_op jit(solution)/shard_map/ppermute | solution.py:277
  176.9 5.1 %collective-permute-start.22 = (bf16[512,2560]{1,0:T(8,128)(2,1)S(1)}, bf16[512,2560]{1,0:T(8,128)(2,1)}, u32[]{:S(2)}, u32[]{:S(2)}) collective-permute-start(bf16[512,2560]{1,0:T(8,128)(2,1)S(1)} %constant_dynamic-update-slice_fusion.refs_3_), channel_id=1, source_target_pairs={{0,1},{1,0},{2,3},{3,2},{4,5},{5,4},{6,7},{7,6},{8,9},{9,8},{10,11... | collective-permute-start | bytes 7864328 | tf_op jit(solution)/shard_map/ppermute | solution.py:280
  177.0 59.4 %collective-permute-start.25 = (bf16[512,384]{1,0:T(8,128)(2,1)S(1)}, bf16[512,384]{1,0:T(8,128)(2,1)S(1)}, u32[]{:S(2)}, u32[]{:S(2)}) collective-permute-start(bf16[512,384]{1,0:T(8,128)(2,1)S(1)} %copy-done.18), channel_id=1, source_target_pairs={{0,4},{2,6},{4,0},{6,2},{8,12},{10,14},{12,8},{14,10},{16,20},{18,... | collective-permute-start | bytes 1179656 | tf_op jit(solution)/shard_map/ppermute | solution.py:277
  177.1 46.1 %collective-permute-start.23 = (bf16[512,384]{1,0:T(8,128)(2,1)}, bf16[512,384]{1,0:T(8,128)(2,1)S(1)}, u32[]{:S(2)}, u32[]{:S(2)}) collective-permute-start(bf16[512,384]{1,0:T(8,128)(2,1)} %get-tuple-element.50), channel_id=1, source_target_pairs={{0,2},{2,0},{4,6},{6,4},{8,10},{10,8},{12,14},{14,12},{16,18},{18,... | collective-permute-start | bytes 1179656 | tf_op jit(solution)/shard_map/ppermute | solution.py:277
  193.5 42.9 %collective-permute-start.27 = (bf16[512,384]{1,0:T(8,128)(2,1)}, bf16[512,384]{1,0:T(8,128)(2,1)S(1)}, u32[]{:S(2)}, u32[]{:S(2)}) collective-permute-start(bf16[512,384]{1,0:T(8,128)(2,1)} %shard_map.74), channel_id=1, source_target_pairs={{0,6},{2,4},{4,2},{6,0},{8,14},{10,12},{12,10},{14,8},{16,22},{18,... | collective-permute-start | bytes 1179656 | tf_op jit(solution)/shard_map/ppermute | solution.py:277
  218.2 18.1 %collective-permute-start.24 = (bf16[512,256]{1,0:T(8,128)(2,1)}, bf16[512,256]{1,0:T(8,128)(2,1)S(1)}, u32[]{:S(2)}, u32[]{:S(2)}) collective-permute-start(bf16[512,256]{1,0:T(8,128)(2,1)} %get-tuple-element.51), channel_id=1, source_target_pairs={{0,2},{2,0},{4,6},{6,4},{8,10},{10,8},{12,14},{14,12},{16,18},{18,... | collective-permute-start | bytes 786440 | tf_op jit(solution)/shard_map/ppermute | solution.py:277
  219.0 17.4 %collective-permute-start.26 = (bf16[512,256]{1,0:T(8,128)(2,1)}, bf16[512,256]{1,0:T(8,128)(2,1)S(1)}, u32[]{:S(2)}, u32[]{:S(2)}) collective-permute-start(bf16[512,256]{1,0:T(8,128)(2,1)} %get-tuple-element.52), channel_id=1, source_target_pairs={{0,4},{2,6},{4,0},{6,2},{8,12},{10,14},{12,8},{14,10},{16,20},{18,... | collective-permute-start | bytes 786440 | tf_op jit(solution)/shard_map/ppermute | solution.py:277
  223.2 13.2 %collective-permute-start.28 = (bf16[512,256]{1,0:T(8,128)(2,1)}, bf16[512,256]{1,0:T(8,128)(2,1)S(1)}, u32[]{:S(2)}, u32[]{:S(2)}) collective-permute-start(bf16[512,256]{1,0:T(8,128)(2,1)} %get-tuple-element.48), channel_id=1, source_target_pairs={{0,6},{2,4},{4,2},{6,0},{8,14},{10,12},{12,10},{14,8},{16,22},{18,... | collective-permute-start | bytes 786440 | tf_op jit(solution)/shard_map/ppermute | solution.py:277
  (18 other events, 225.2 us)
Sparse Core Ops, SparseCore 0:
  39.3 72.4 all-gather.2
  138.5 51.5 all-gather.4
where the time goes:
time: 250 us; the launch traced here: 248 us
  waiting for transfers between devices  85.2 us (34%)
  Pallas kernels  83 us (33%)
  starting transfers between devices  37.2 us (15%)
  local copies, waits for them, and re-layouts  16.7 us (7%)
  between operations  13.8 us (6%)
  other arithmetic  11.8 us (5%)
    ppermute x22, waiting for transfers between devices, swapped(): lax.ppermute(block, 'ctx', [(i, i ^ distance) for i in range(devices)])  81.2 us
    pallas_call x4, Pallas kernels, attend(): pl.pallas_call(kernel, out_shape=[jax.ShapeDtypeStruct((rows, columns), j...  79.6 us
    ppermute x22, starting transfers between devices, swapped(): lax.ppermute(block, 'ctx', [(i, i ^ distance) for i in range(devices)])  29.3 us
    ppermute x2, starting transfers between devices, planar(): lax.ppermute(array, 'ctx', hop)  7.1 us
  transfers between devices with their start and end apart: 31, of which 9 were waited for; matrix products, arithmetic and copies ran while one was open for 11% of the time, Pallas kernels for 32%

commit v1 on v0

--- a/solution.py
+++ b/solution.py
@@ -292,11 +292,10 @@
 
     marks_own = marks_of(doc_start, tile_mask)
     w_first = [columns_for(w_query, d, cuts[0][0], cuts[0][1] - cuts[0][0], q_width, 1) for d in range(group)]
+    kv_own = after([cache_keys, cache_values], *w_first)
     w_first = w_first[:1] + [swapped(w_first[d], d) for d in far]
     hop = [(i, i + group) for i in range(devices - group)]
-    kv_before = [lax.ppermute(array, "ctx", hop) for array in (cache_keys, cache_values)]
-    (marks_sent,) = after([marks_own], *w_first)
-    marks = [marks_own] + [swapped(marks_sent, d) for d in far]
+    kv_before = [lax.ppermute(array, "ctx", hop) for array in kv_own]
 
     float_tokens = tokens.astype(jnp.float32)
     squares = jnp.sum(float_tokens * float_tokens, axis=-1)
@@ -305,8 +304,13 @@
     gain = lax.dynamic_slice_in_dim(norm_gain, core * width, width, 0)
     normed = (float_tokens * inverse[:, None] * gain).astype(jnp.bfloat16)
 
-    w_first = after(w_first, *kv_before)
-    w_chunks = [lax.all_gather(jnp.stack(w_first), "ctx", axis=0, tiled=True, axis_index_groups=lines)]
+    w_second = [columns_for(w_query, d, cuts[1][0], cuts[1][1] - cuts[1][0], q_width, 1) for d in range(group)]
+    w_second = after(w_second, *w_first)
+    w_second = w_second[:1] + [swapped(w_second[d], d) for d in far]
+    w_stack = jnp.stack(after(w_first, *kv_before))
+    w_chunks = [lax.all_gather(w_stack, "ctx", axis=0, tiled=True, axis_index_groups=lines)]
+    (marks_sent,) = after([marks_own], w_stack)
+    marks = [marks_own] + [swapped(marks_sent, d) for d in far]
 
     def kv_for(d):
         arrays = (*kv_before, cache_keys, cache_values)
@@ -314,14 +318,11 @@
             2, 2, tok_rows, kv_width
         )
 
-    w_second = [columns_for(w_query, d, cuts[1][0], cuts[1][1] - cuts[1][0], q_width, 1) for d in range(group)]
-    (normed,) = after([normed], *marks)
-    w_second = after(w_second, *marks)
-    from_x, from_y = swapped(normed, 1), swapped(normed, 2)
-    w_second = w_second[:1] + [swapped(w_second[d], d) for d in far]
-    mine_other = other_core(normed)
     kv_cut = [kv_for(d) for d in range(group)]
     kv_parts = kv_cut[:1] + [swapped(kv_cut[d], d) for d in far]
+    (normed,) = after([normed], *marks, *kv_cut, *w_second)
+    from_x, from_y = swapped(normed, 1), swapped(normed, 2)
+    mine_other = other_core(normed)
     (w_after,) = after([jnp.stack(w_second)], *kv_parts)
     w_chunks.append(lax.all_gather(w_after, "ctx", axis=0, tiled=True, axis_index_groups=lines))
 

time: 250 us -> 253 us (1.012)
  the two profiles are of different devices: /device:TPU:10 before, /device:TPU:0 now
where the time goes in v1:
time: 253 us; the launch traced here: 252 us
  waiting for transfers between devices  91.7 us (36%)
  Pallas kernels  75.1 us (30%)
  starting transfers between devices  34 us (13%)
  other arithmetic  19.2 us (8%)
  local copies, waits for them, and re-layouts  17.9 us (7%)
  between operations  13.7 us (5%)
    ppermute x22, waiting for transfers between devices, swapped(): lax.ppermute(block, 'ctx', [(i, i ^ distance) for i in range(devices)])  81.3 us
    pallas_call x4, Pallas kernels, attend(): pl.pallas_call(kernel, out_shape=[jax.ShapeDtypeStruct((rows, columns), j...  71.7 us
    ppermute x22, starting transfers between devices, swapped(): lax.ppermute(block, 'ctx', [(i, i ^ distance) for i in range(devices)])  25.6 us
    ppermute x2, starting transfers between devices, planar(): kv_before = [lax.ppermute(array, 'ctx', hop) for array in kv_own]  7.73 us
    another operation x4, other arithmetic, kv_for(): jnp.stack([columns_for(array, d, 0, kv_width, kv_width, 1) for array in a...  6.6 us
    ppermute x2, waiting for transfers between devices, planar(): kv_before = [lax.ppermute(array, 'ctx', hop) for array in kv_own]  5.68 us
  transfers between devices with their start and end apart: 31, of which 10 were waited for; matrix products, arithmetic and copies ran while one was open for 13% of the time, Pallas kernels for 29%

profile of v1, /device:TPU:0, one launch (start us, length us, event | category | flops | bytes accessed | tf_op | source)
XLA Modules:
  0.0 251.6 jit_solution(6044273053383116146)
XLA Ops:
  6.5 2.3 constant_dynamic-slice_fusion.4
  8.8 2.9 %collective-permute-start = (bf16[320,384]{1,0:T(8,128)(2,1)}, bf16[320,384]{1,0:T(8,128)(2,1)}, u32[]{:S(2)}, u32[]{:S(2)}) collective-permute-start(bf16[320,384]{1,0:T(8,128)(2,1)} %get-tuple-element.63), channel_id=1, source_target_pairs={{0,2},{2,0},{4,6},{6,4},{8,10},{10,8},{12,14},{14,12},{16,18},{18,... | collective-permute-start | bytes 737288 | tf_op jit(solution)/shard_map/ppermute | solution.py:277
  11.7 1.5 collective-permute-start.1
  13.3 5.0 %collective-permute-start.3 = (bf16[512,512]{1,0:T(8,128)(2,1)}, bf16[512,512]{1,0:T(8,128)(2,1)}, u32[]{:S(2)}, u32[]{:S(2)}) collective-permute-start(bf16[512,512]{1,0:T(8,128)(2,1)} %param.10), channel_id=1, source_target_pairs={{0,8},{2,10},{4,12},{6,14},{8,16},{10,18},{12,20},{14,22},{16,24},... | collective-permute-start | bytes 1572872 | tf_op jit(solution)/shard_map/ppermute | solution.py:298
  18.3 2.9 %fusion = f32[512]{0:T(512)} fusion(bf16[512,2560]{1,0:T(8,128)(2,1)} %param.7), kind=kLoop, calls=%fused_computation.2 | loop fusion | flops 3931648 | bytes 2623488 | tf_op jit(solution)/shard_map/reduce_sum | solution.py:301
  21.9 2.0 constant_dynamic-slice_fusion
  23.8 2.1 dynamic-slice_bitcast_fusion
  28.0 2.7 %collective-permute-start.4 = (bf16[512,512]{1,0:T(8,128)(2,1)}, bf16[512,512]{1,0:T(8,128)(2,1)S(1)}, u32[]{:S(2)}, u32[]{:S(2)}) collective-permute-start(bf16[512,512]{1,0:T(8,128)(2,1)} %param.11), channel_id=1, source_target_pairs={{0,8},{2,10},{4,12},{6,14},{8,16},{10,18},{12,20},{14,22},{16,24},... | collective-permute-start | bytes 1572872 | tf_op jit(solution)/shard_map/ppermute | solution.py:298
  31.5 2.2 fusion.2.refs_7_.refs_3_
  33.6 1.6 collective-permute-start.9
  37.2 5.7 %collective-permute-done.4 = bf16[512,512]{1,0:T(8,128)(2,1)S(1)} collective-permute-done((bf16[512,512]{1,0:T(8,128)(2,1)}, bf16[512,512]{1,0:T(8,128)(2,1)S(1)}, u32[]{:S(2)}, u32[]{:S(2)}) %collective-permute-start.4) | collective-permute-done | bytes 524320 | tf_op jit(solution)/shard_map/ppermute | solution.py:298
  42.9 2.3 pad_maximum_fusion
  49.6 2.0 pad_maximum_fusion.3
  51.6 1.9 pad_maximum_fusion.4
  53.5 1.9 pad_maximum_fusion.5
  56.7 3.1 %collective-permute-done.8 = s32[6,128]{1,0:T(8,128)S(1)} collective-permute-done((s32[6,128]{1,0:T(8,128)S(1)}, s32[6,128]{1,0:T(8,128)S(1)}, u32[]{:S(2)}, u32[]{:S(2)}) %collective-permute-start.8) | collective-permute-done | bytes 3104 | tf_op jit(solution)/shard_map/ppermute | solution.py:277
  62.4 1.6 collective-permute-start.15
  64.4 2.0 pad_maximum_fusion.1
  66.4 64.5 %collective-permute-done.14.refs_11_.refs_7_ = bf16[2,2,512,128]{3,2,1,0:T(8,128)(2,1)S(1)} collective-permute-done((bf16[2,2,512,128]{3,2,1,0:T(8,128)(2,1)}, bf16[2,2,512,128]{3,2,1,0:T(8,128)(2,1)S(1)}, u32[]{:S(2)}, u32[]{:S(2)}) %collective-permute-start.14) | collective-permute-done | bytes 524320 | tf_op jit(solution)/shard_map/ppermute | solution.py:277
  130.9 8.5 %collective-permute-done.15.refs_12_.refs_8_ = bf16[2,2,512,128]{3,2,1,0:T(8,128)(2,1)} collective-permute-done((bf16[2,2,512,128]{3,2,1,0:T(8,128)(2,1)}, bf16[2,2,512,128]{3,2,1,0:T(8,128)(2,1)}, u32[]{:S(2)}, u32[]{:S(2)}) %collective-permute-start.15) | collective-permute-done | bytes 524320 | tf_op jit(solution)/shard_map/ppermute | solution.py:277
  140.0 2.5 slice.6
  142.5 2.5 slice.7
  148.5 26.2 %shard_map.73 = (bf16[512,384]{1,0:T(8,128)(2,1)}, bf16[512,384]{1,0:T(8,128)(2,1)}, bf16[512,384]{1,0:T(8,128)(2,1)}) custom-call(s32[3]{0:T(128)} %pad_add_fusion.3.refs_0_.info_ref, s32[3,6,128]{2,1,0:T(8,128)} %get-tuple-element.82.refs_1_.refs_2_, s32[3,6,128]{2,1,0:T(8,128)} %get-tuple-element.82.refs_1_.refs_2_, ...), custom_call_target="tpu_custom_call" | custom-call | flops 8455716864 | bytes 22937600 | tf_op jit(solution)/shard_map/pallas_call | solution.py:229
  180.3 2.4 collective-permute-start.25
  182.7 1.6 collective-permute-start.23
  185.3 15.0 %shard_map.74 = bf16[512,384]{1,0:T(8,128)(2,1)} custom-call(s32[3]{0:T(128)} %pad_add_fusion.3.refs_0_.info_ref, s32[1,6,128]{2,1,0:T(8,128)} %bitcast.60, s32[1,6,128]{2,1,0:T(8,128)} %bitcast.61, bf16[512,2560]{1,0:T(8,128)(2,1)} %copy-done.2, bf16[512,2560]{1,0:T(8,128)(2,1)} %collective-permute-done.22.refs_4_, ...), custom_call_target="tpu_custom_call" | custom-call | flops 2818572288 | bytes 11665408 | tf_op jit(solution)/shard_map/pallas_call | solution.py:229
  200.4 3.4 %all-gather.5.cloned.1.call-done.refs_9_.refs_5_ = bf16[16,320,256]{2,1,0:T(8,128)(2,1)} async-done(((bf16[4,320,256]{2,1,0:T(8,128)(2,1)}), bf16[16,320,256]{2,1,0:T(8,128)(2,1)}) %all-gather.5.cloned.1.call-update) | async-done | bytes 2621456 | tf_op jit(solution)/shard_map/all_gather | solution.py:327
  203.8 22.3 %shard_map.75 = (bf16[512,256]{1,0:T(8,128)(2,1)}, bf16[512,256]{1,0:T(8,128)(2,1)}, bf16[512,256]{1,0:T(8,128)(2,1)}) custom-call(s32[3]{0:T(128)} %pad_add_fusion.3.refs_0_.info_ref, s32[3,6,128]{2,1,0:T(8,128)} %get-tuple-element.81.refs_1_.refs_2_, s32[3,6,128]{2,1,0:T(8,128)} %get-tuple-element.81.refs_1_.refs_2_, bf16[512,2560]{1,0:T(8,128)(2,1)} %copy-done.2, ...), custom_call_target="tpu_custom_call" | custom-call | flops 5637144576 | bytes 21233664 | tf_op jit(solution)/shard_map/pallas_call | solution.py:229
  226.9 2.7 %collective-permute-start.28 = (bf16[512,256]{1,0:T(8,128)(2,1)}, bf16[512,256]{1,0:T(8,128)(2,1)S(1)}, u32[]{:S(2)}, u32[]{:S(2)}) collective-permute-start(bf16[512,256]{1,0:T(8,128)(2,1)} %get-tuple-element.52), channel_id=1, source_target_pairs={{0,6},{2,4},{4,2},{6,0},{8,14},{10,12},{12,10},{14,8},{16,22},{18,... | collective-permute-start | bytes 786440 | tf_op jit(solution)/shard_map/ppermute | solution.py:277
  229.7 8.2 %shard_map.76.refs_1_ = bf16[512,256]{1,0:T(8,128)(2,1)} custom-call(s32[3]{0:T(128)} %pad_add_fusion.3.refs_0_.info_ref, s32[1,6,128]{2,1,0:T(8,128)} %get-tuple-element.84.refs_1_.refs_2_, s32[1,6,128]{2,1,0:T(8,128)} %get-tuple-element.84.refs_1_.refs_2_, bf16[512,2560]{1,0:T(8,128)(2,1)} %fusion.2.refs_7_.refs_3_, ...), custom_call_target="tpu_custom_call" | custom-call | flops 1879048192 | bytes 10223616 | tf_op jit(solution)/shard_map/pallas_call | solution.py:229
  238.0 2.5 %collective-permute-done.26.refs_5_ = bf16[512,256]{1,0:T(8,128)(2,1)S(1)} collective-permute-done((bf16[512,256]{1,0:T(8,128)(2,1)}, bf16[512,256]{1,0:T(8,128)(2,1)S(1)}, u32[]{:S(2)}, u32[]{:S(2)}) %collective-permute-start.26) | collective-permute-done | bytes 262176 | tf_op jit(solution)/shard_map/ppermute | solution.py:277
  241.4 3.4 %shard_map.77 = bf16[512,2560]{1,0:T(8,128)(2,1)} custom-call(s32[3]{0:T(128)} %pad_add_fusion.3.refs_0_.info_ref, bf16[512,384]{1,0:T(8,128)(2,1)} %get-tuple-element.46.refs_0_, bf16[512,256]{1,0:T(8,128)(2,1)} %shard_map.76.refs_1_, bf16[512,384]{1,0:T(8,128)(2,1)} %copy-done.8, bf16[512,256]{1,0:T(8,128)(2,1)} %copy-done.10, bf16[512,384]{1,0:T(8,128)(2,1)} %copy-done.7, ...), custom_call_target="tpu_custom_call" | custom-call | bytes 5242880 | tf_op jit(solution)/shard_map/pallas_call | solution.py:365
  (106 shorter events, 26.5 us)
Async XLA Ops:
  6.5 142.0 %all-gather.3.cloned.1.call-start = ((), (), s32[]{:S(2)}) async-start(), calls=%async_computation | async-start | bytes 4915200 | tf_op jit(solution)/shard_map/all_gather | solution.py:311
  8.8 24.8 %collective-permute-start = (bf16[320,384]{1,0:T(8,128)(2,1)}, bf16[320,384]{1,0:T(8,128)(2,1)}, u32[]{:S(2)}, u32[]{:S(2)}) collective-permute-start(bf16[320,384]{1,0:T(8,128)(2,1)} %get-tuple-element.63), channel_id=1, source_target_pairs={{0,2},{2,0},{4,6},{6,4},{8,10},{10,8},{12,14},{14,12},{16,18},{18,... | collective-permute-start | bytes 737288 | tf_op jit(solution)/shard_map/ppermute | solution.py:277
  11.7 21.9 %collective-permute-start.1 = (bf16[320,384]{1,0:T(8,128)(2,1)}, bf16[320,384]{1,0:T(8,128)(2,1)}, u32[]{:S(2)}, u32[]{:S(2)}) collective-permute-start(bf16[320,384]{1,0:T(8,128)(2,1)} %get-tuple-element.62), channel_id=1, source_target_pairs={{0,4},{2,6},{4,0},{6,2},{8,12},{10,14},{12,8},{14,10},{16,20},{18,... | collective-permute-start | bytes 737288 | tf_op jit(solution)/shard_map/ppermute | solution.py:277
  13.3 20.4 %collective-permute-start.2 = (bf16[320,384]{1,0:T(8,128)(2,1)}, bf16[320,384]{1,0:T(8,128)(2,1)}, u32[]{:S(2)}, u32[]{:S(2)}) collective-permute-start(bf16[320,384]{1,0:T(8,128)(2,1)} %get-tuple-element.61), channel_id=1, source_target_pairs={{0,6},{2,4},{4,2},{6,0},{8,14},{10,12},{12,10},{14,8},{16,22},{18,... | collective-permute-start | bytes 737288 | tf_op jit(solution)/shard_map/ppermute | solution.py:277
  13.3 23.9 %collective-permute-start.3 = (bf16[512,512]{1,0:T(8,128)(2,1)}, bf16[512,512]{1,0:T(8,128)(2,1)}, u32[]{:S(2)}, u32[]{:S(2)}) collective-permute-start(bf16[512,512]{1,0:T(8,128)(2,1)} %param.10), channel_id=1, source_target_pairs={{0,8},{2,10},{4,12},{6,14},{8,16},{10,18},{12,20},{14,22},{16,24},... | collective-permute-start | bytes 1572872 | tf_op jit(solution)/shard_map/ppermute | solution.py:298
  21.2 6.9 %collective-permute-start.7 = (f32[512]{0:T(512)}, f32[512]{0:T(512)}, u32[]{:S(2)}, u32[]{:S(2)}) collective-permute-start(f32[512]{0:T(512)} %fusion), channel_id=1, source_target_pairs={{0,1},{1,0},{2,3},{3,2},{4,5},{5,4},{6,7},{7,6},{8,9},{9,8},{10,11... | collective-permute-start | bytes 6152 | tf_op jit(solution)/shard_map/ppermute | solution.py:280
  28.0 14.8 %collective-permute-start.4 = (bf16[512,512]{1,0:T(8,128)(2,1)}, bf16[512,512]{1,0:T(8,128)(2,1)S(1)}, u32[]{:S(2)}, u32[]{:S(2)}) collective-permute-start(bf16[512,512]{1,0:T(8,128)(2,1)} %param.11), channel_id=1, source_target_pairs={{0,8},{2,10},{4,12},{6,14},{8,16},{10,18},{12,20},{14,22},{16,24},... | collective-permute-start | bytes 1572872 | tf_op jit(solution)/shard_map/ppermute | solution.py:298
  33.6 21.7 %collective-permute-start.9 = (bf16[320,256]{1,0:T(8,128)(2,1)}, bf16[320,256]{1,0:T(8,128)(2,1)}, u32[]{:S(2)}, u32[]{:S(2)}) collective-permute-start(bf16[320,256]{1,0:T(8,128)(2,1)} %get-tuple-element.39), channel_id=1, source_target_pairs={{0,2},{2,0},{4,6},{6,4},{8,10},{10,8},{12,14},{14,12},{16,18},{18,... | collective-permute-start | bytes 491528 | tf_op jit(solution)/shard_map/ppermute | solution.py:277
  35.2 21.5 %collective-permute-start.10 = (bf16[320,256]{1,0:T(8,128)(2,1)}, bf16[320,256]{1,0:T(8,128)(2,1)}, u32[]{:S(2)}, u32[]{:S(2)}) collective-permute-start(bf16[320,256]{1,0:T(8,128)(2,1)} %get-tuple-element.40), channel_id=1, source_target_pairs={{0,4},{2,6},{4,0},{6,2},{8,12},{10,14},{12,8},{14,10},{16,20},{18,... | collective-permute-start | bytes 491528 | tf_op jit(solution)/shard_map/ppermute | solution.py:277
  36.7 20.0 %collective-permute-start.11 = (bf16[320,256]{1,0:T(8,128)(2,1)}, bf16[320,256]{1,0:T(8,128)(2,1)}, u32[]{:S(2)}, u32[]{:S(2)}) collective-permute-start(bf16[320,256]{1,0:T(8,128)(2,1)} %get-tuple-element.41), channel_id=1, source_target_pairs={{0,6},{2,4},{4,2},{6,0},{8,14},{10,12},{12,10},{14,8},{16,22},{18,... | collective-permute-start | bytes 491528 | tf_op jit(solution)/shard_map/ppermute | solution.py:277
  45.2 11.5 %collective-permute-start.5 = (s32[6,128]{1,0:T(8,128)}, s32[6,128]{1,0:T(8,128)S(1)}, u32[]{:S(2)}, u32[]{:S(2)}) collective-permute-start(s32[6,128]{1,0:T(8,128)} %get-tuple-element.37), channel_id=1, source_target_pairs={{0,4},{2,6},{4,0},{6,2},{8,12},{10,14},{12,8},{14,10},{16,20},{18,... | collective-permute-start | bytes 9224 | tf_op jit(solution)/shard_map/ppermute | solution.py:277
  46.7 10.0 %collective-permute-start.6 = (s32[6,128]{1,0:T(8,128)}, s32[6,128]{1,0:T(8,128)S(1)}, u32[]{:S(2)}, u32[]{:S(2)}) collective-permute-start(s32[6,128]{1,0:T(8,128)} %get-tuple-element.37), channel_id=1, source_target_pairs={{0,2},{2,0},{4,6},{6,4},{8,10},{10,8},{12,14},{14,12},{16,18},{18,... | collective-permute-start | bytes 9224 | tf_op jit(solution)/shard_map/ppermute | solution.py:277
  48.2 155.6 %all-gather.5.cloned.1.call-start = ((), (), s32[]{:S(2)}) async-start(), calls=%async_computation.1 | async-start | bytes 3276800 | tf_op jit(solution)/shard_map/all_gather | solution.py:327
  55.4 4.5 %collective-permute-start.8 = (s32[6,128]{1,0:T(8,128)S(1)}, s32[6,128]{1,0:T(8,128)S(1)}, u32[]{:S(2)}, u32[]{:S(2)}) collective-permute-start(s32[6,128]{1,0:T(8,128)S(1)} %copy-done.19), channel_id=1, source_target_pairs={{0,6},{2,4},{4,2},{6,0},{8,14},{10,12},{12,10},{14,8},{16,22},{18,... | collective-permute-start | bytes 9224 | tf_op jit(solution)/shard_map/ppermute | solution.py:277
  59.9 87.8 %copy-start.14 = (s32[6,128]{1,0:T(8,128)}, s32[6,128]{1,0:T(8,128)S(1)}, u32[]{:S(2)}) copy-start(s32[6,128]{1,0:T(8,128)S(1)} %collective-permute-done.8) | copy-start | bytes 9220
  59.9 79.6 %collective-permute-start.12 = (bf16[512,2560]{1,0:T(8,128)(2,1)S(1)}, bf16[512,2560]{1,0:T(8,128)(2,1)}, u32[]{:S(2)}, u32[]{:S(2)}) collective-permute-start(bf16[512,2560]{1,0:T(8,128)(2,1)S(1)} %copy-done.1), channel_id=1, source_target_pairs={{0,2},{2,0},{4,6},{6,4},{8,10},{10,8},{12,14},{14,12},{16,18},{18,... | collective-permute-start | bytes 7864328 | tf_op jit(solution)/shard_map/ppermute | solution.py:277
  60.4 79.1 %collective-permute-start.13 = (bf16[512,2560]{1,0:T(8,128)(2,1)S(1)}, bf16[512,2560]{1,0:T(8,128)(2,1)}, u32[]{:S(2)}, u32[]{:S(2)}) collective-permute-start(bf16[512,2560]{1,0:T(8,128)(2,1)S(1)} %copy-done.1), channel_id=1, source_target_pairs={{0,4},{2,6},{4,0},{6,2},{8,12},{10,14},{12,8},{14,10},{16,20},{18,... | collective-permute-start | bytes 7864328 | tf_op jit(solution)/shard_map/ppermute | solution.py:277
  60.9 70.0 %collective-permute-start.14 = (bf16[2,2,512,128]{3,2,1,0:T(8,128)(2,1)}, bf16[2,2,512,128]{3,2,1,0:T(8,128)(2,1)S(1)}, u32[]{:S(2)}, u32[]{:S(2)}) collective-permute-start(bf16[2,2,512,128]{3,2,1,0:T(8,128)(2,1)} %bitcast.20), channel_id=1, source_target_pairs={{0,2},{2,0},{4,6},{6,4},{8,10},{10,8},{12,14},{14,12},{16,18},{18,... | collective-permute-start | bytes 1572872 | tf_op jit(solution)/shard_map/ppermute | solution.py:277
  62.4 77.1 %collective-permute-start.15 = (bf16[2,2,512,128]{3,2,1,0:T(8,128)(2,1)}, bf16[2,2,512,128]{3,2,1,0:T(8,128)(2,1)}, u32[]{:S(2)}, u32[]{:S(2)}) collective-permute-start(bf16[2,2,512,128]{3,2,1,0:T(8,128)(2,1)} %bitcast.25), channel_id=1, source_target_pairs={{0,4},{2,6},{4,0},{6,2},{8,12},{10,14},{12,8},{14,10},{16,20},{18,... | collective-permute-start | bytes 1572872 | tf_op jit(solution)/shard_map/ppermute | solution.py:277
  63.9 75.5 %collective-permute-start.16 = (bf16[2,2,512,128]{3,2,1,0:T(8,128)(2,1)}, bf16[2,2,512,128]{3,2,1,0:T(8,128)(2,1)}, u32[]{:S(2)}, u32[]{:S(2)}) collective-permute-start(bf16[2,2,512,128]{3,2,1,0:T(8,128)(2,1)} %bitcast.30), channel_id=1, source_target_pairs={{0,6},{2,4},{4,2},{6,0},{8,14},{10,12},{12,10},{14,8},{16,22},{18,... | collective-permute-start | bytes 1572872 | tf_op jit(solution)/shard_map/ppermute | solution.py:277
  130.9 17.4 %collective-permute-start.19 = (bf16[512,2560]{1,0:T(8,128)(2,1)S(1)}, bf16[512,2560]{1,0:T(8,128)(2,1)}, u32[]{:S(2)}, u32[]{:S(2)}) collective-permute-start(bf16[512,2560]{1,0:T(8,128)(2,1)S(1)} %copy-done.1), channel_id=1, source_target_pairs={{0,1},{1,0},{2,3},{3,2},{4,5},{5,4},{6,7},{7,6},{8,9},{9,8},{10,11... | collective-permute-start | bytes 7864328 | tf_op jit(solution)/shard_map/ppermute | solution.py:280
  139.5 8.8 %collective-permute-start.17 = (bf16[512,2560]{1,0:T(8,128)(2,1)}, bf16[512,2560]{1,0:T(8,128)(2,1)}, u32[]{:S(2)}, u32[]{:S(2)}) collective-permute-start(bf16[512,2560]{1,0:T(8,128)(2,1)} %collective-permute-done.13.refs_3_.refs_5_), channel_id=1, source_target_pairs={{0,1},{1,0},{2,3},{3,2},{4,5},{5,4},{6,7},{7,6},{8,9},{9,8},{10,11... | collective-permute-start | bytes 7864328 | tf_op jit(solution)/shard_map/ppermute | solution.py:280
  139.5 9.0 %collective-permute-start.18 = (bf16[512,2560]{1,0:T(8,128)(2,1)}, bf16[512,2560]{1,0:T(8,128)(2,1)}, u32[]{:S(2)}, u32[]{:S(2)}) collective-permute-start(bf16[512,2560]{1,0:T(8,128)(2,1)} %collective-permute-done.12.refs_5_.refs_7_), channel_id=1, source_target_pairs={{0,1},{1,0},{2,3},{3,2},{4,5},{5,4},{6,7},{7,6},{8,9},{9,8},{10,11... | collective-permute-start | bytes 7864328 | tf_op jit(solution)/shard_map/ppermute | solution.py:280
  145.0 31.1 %collective-permute-start.20 = (bf16[512,1280]{1,0:T(8,128)(2,1)}, bf16[512,1280]{1,0:T(8,128)(2,1)}, u32[]{:S(2)}, u32[]{:S(2)}) collective-permute-start(bf16[512,1280]{1,0:T(8,128)(2,1)} %slice.6), channel_id=1, source_target_pairs={{0,2},{2,0},{4,6},{6,4},{8,10},{10,8},{12,14},{14,12},{16,18},{18,... | collective-permute-start | bytes 3932168 | tf_op jit(solution)/shard_map/ppermute | solution.py:277
  146.5 30.8 %collective-permute-start.21 = (bf16[512,1280]{1,0:T(8,128)(2,1)}, bf16[512,1280]{1,0:T(8,128)(2,1)}, u32[]{:S(2)}, u32[]{:S(2)}) collective-permute-start(bf16[512,1280]{1,0:T(8,128)(2,1)} %slice.7), channel_id=1, source_target_pairs={{0,4},{2,6},{4,0},{6,2},{8,12},{10,14},{12,8},{14,10},{16,20},{18,... | collective-permute-start | bytes 3932168 | tf_op jit(solution)/shard_map/ppermute | solution.py:277
  180.2 5.1 %collective-permute-start.22 = (bf16[512,2560]{1,0:T(8,128)(2,1)S(1)}, bf16[512,2560]{1,0:T(8,128)(2,1)}, u32[]{:S(2)}, u32[]{:S(2)}) collective-permute-start(bf16[512,2560]{1,0:T(8,128)(2,1)S(1)} %constant_dynamic-update-slice_fusion.refs_3_), channel_id=1, source_target_pairs={{0,1},{1,0},{2,3},{3,2},{4,5},{5,4},{6,7},{7,6},{8,9},{9,8},{10,11... | collective-permute-start | bytes 7864328 | tf_op jit(solution)/shard_map/ppermute | solution.py:280
  180.3 57.7 %collective-permute-start.25 = (bf16[512,384]{1,0:T(8,128)(2,1)S(1)}, bf16[512,384]{1,0:T(8,128)(2,1)S(1)}, u32[]{:S(2)}, u32[]{:S(2)}) collective-permute-start(bf16[512,384]{1,0:T(8,128)(2,1)S(1)} %copy-done.22), channel_id=1, source_target_pairs={{0,4},{2,6},{4,0},{6,2},{8,12},{10,14},{12,8},{14,10},{16,20},{18,... | collective-permute-start | bytes 1179656 | tf_op jit(solution)/shard_map/ppermute | solution.py:277
  182.7 44.3 %collective-permute-start.23 = (bf16[512,384]{1,0:T(8,128)(2,1)}, bf16[512,384]{1,0:T(8,128)(2,1)S(1)}, u32[]{:S(2)}, u32[]{:S(2)}) collective-permute-start(bf16[512,384]{1,0:T(8,128)(2,1)} %get-tuple-element.54), channel_id=1, source_target_pairs={{0,2},{2,0},{4,6},{6,4},{8,10},{10,8},{12,14},{14,12},{16,18},{18,... | collective-permute-start | bytes 1179656 | tf_op jit(solution)/shard_map/ppermute | solution.py:277
  200.3 40.2 %collective-permute-start.27 = (bf16[512,384]{1,0:T(8,128)(2,1)}, bf16[512,384]{1,0:T(8,128)(2,1)S(1)}, u32[]{:S(2)}, u32[]{:S(2)}) collective-permute-start(bf16[512,384]{1,0:T(8,128)(2,1)} %shard_map.74), channel_id=1, source_target_pairs={{0,6},{2,4},{4,2},{6,0},{8,14},{10,12},{12,10},{14,8},{16,22},{18,... | collective-permute-start | bytes 1179656 | tf_op jit(solution)/shard_map/ppermute | solution.py:277
  226.1 11.8 %collective-permute-start.24 = (bf16[512,256]{1,0:T(8,128)(2,1)}, bf16[512,256]{1,0:T(8,128)(2,1)S(1)}, u32[]{:S(2)}, u32[]{:S(2)}) collective-permute-start(bf16[512,256]{1,0:T(8,128)(2,1)} %get-tuple-element.55), channel_id=1, source_target_pairs={{0,2},{2,0},{4,6},{6,4},{8,10},{10,8},{12,14},{14,12},{16,18},{18,... | collective-permute-start | bytes 786440 | tf_op jit(solution)/shard_map/ppermute | solution.py:277
  226.9 13.6 %collective-permute-start.26 = (bf16[512,256]{1,0:T(8,128)(2,1)}, bf16[512,256]{1,0:T(8,128)(2,1)S(1)}, u32[]{:S(2)}, u32[]{:S(2)}) collective-permute-start(bf16[512,256]{1,0:T(8,128)(2,1)} %get-tuple-element.56), channel_id=1, source_target_pairs={{0,4},{2,6},{4,0},{6,2},{8,12},{10,14},{12,8},{14,10},{16,20},{18,... | collective-permute-start | bytes 786440 | tf_op jit(solution)/shard_map/ppermute | solution.py:277
  226.9 13.6 %collective-permute-start.28 = (bf16[512,256]{1,0:T(8,128)(2,1)}, bf16[512,256]{1,0:T(8,128)(2,1)S(1)}, u32[]{:S(2)}, u32[]{:S(2)}) collective-permute-start(bf16[512,256]{1,0:T(8,128)(2,1)} %get-tuple-element.52), channel_id=1, source_target_pairs={{0,6},{2,4},{4,2},{6,0},{8,14},{10,12},{12,10},{14,8},{16,22},{18,... | collective-permute-start | bytes 786440 | tf_op jit(solution)/shard_map/ppermute | solution.py:277
  (22 other events, 378.7 us)
Sparse Core Ops, SparseCore 0:
  48.3 75.5 all-gather.2
  148.4 55.3 all-gather.4

commit v2 on v1

--- a/solution.py
+++ b/solution.py
@@ -22,7 +22,7 @@
 
 
 def rows_kernel(counts, distances, shapes, info, marks_smem, marks_ref, *refs):
-    parts, kv_count, mask_width = counts
+    parts, kv_count, halves, mask_width = counts
     tok_rows, shard_rows, source_rows = shapes
     n = len(distances)
     token_hbm = [refs[k * parts : (k + 1) * parts] for k in range(n)]
@@ -36,7 +36,6 @@
     heads = columns // HD
     depth = w_ref.shape[0]
     blocks = depth // source_rows
-    halves = kv_hbm[0].shape[0]
     swap = info[1]
     chunk = depth // CHUNKS
     chunks_part = CHUNKS // parts
@@ -66,7 +65,9 @@
     def kv_copy(ref, half, which, place):
         target = pl.ds(pl.multiple_of(KEYS + place * shard_rows, 16), shard_rows)
         return pltpu.make_async_copy(
-            ref.at[half, which], (key_ref, value_ref)[which].at[target], kv_sem.at[place, which]
+            ref.at[pl.ds((half * 2 + which) * shard_rows, shard_rows), :],
+            (key_ref, value_ref)[which].at[target],
+            kv_sem.at[place, which],
         )
 
     def out_copy(k, slot):
@@ -141,9 +142,9 @@
             row_first = rows_first + tile * QUERIES
             end = row_first + QUERIES
             for sub in range(subs):
-                docs_row = marks_ref[k, pl.ds(tile * subs + sub, 1), :].astype(jnp.float32)
+                docs_row = marks_ref[distance, pl.ds(tile * subs + sub, 1), :].astype(jnp.float32)
                 doc_full[sub] = jnp.transpose(jnp.broadcast_to(docs_row, (TILE, TILE))).astype(jnp.int32)
-            first_key = marks_smem[k, tile * subs, 0] - info[0]
+            first_key = marks_smem[distance, tile * subs, 0] - info[0]
             count = (end - first_key + KEYS - 1) // KEYS
 
             def one_block(back, carry):
@@ -163,7 +164,7 @@
                     for m in range(KEYS // TILE):
                         column = lax.min(lax.max(key_tile + m, 0), mask_width - 1)
                         flat = (tile * subs + sub) * mask_width + column
-                        shut = jnp.where(marks_smem[k, doc_rows + flat // TILE, lax.rem(flat, TILE)] == 1, 0, FAR)
+                        shut = jnp.where(marks_smem[distance, doc_rows + flat // TILE, lax.rem(flat, TILE)] == 1, 0, FAR)
                         pieces.append((lane <= causal - m * TILE) & (lane >= docs + (shut - m * TILE)))
                     masks.append(jnp.concatenate(pieces, axis=1))
                 visible = jnp.concatenate(masks, axis=0)
@@ -207,20 +208,20 @@
         out_copy(k, k % 2).wait()
 
 
-def attend(info, marks, distances, token_parts, w_blocks, kv_parts, mask_width):
+def attend(info, marks, distances, token_parts, w_blocks, kv_parts, halves, mask_width):
     n = len(distances)
     parts = len(token_parts[0])
     rows = token_parts[0][0].shape[0]
     source_rows, columns = w_blocks.shape[1:]
     depth = w_blocks.shape[0] * source_rows
     heads = columns // HD
-    shard_rows = kv_parts[0].shape[2]
-    shards = len(kv_parts) * kv_parts[0].shape[0]
+    shard_rows = kv_parts[0].shape[0] // (2 * halves) // TILE * TILE
+    shards = len(kv_parts) * halves
     vmem = pl.BlockSpec(memory_space=pltpu.VMEM)
     smem = pl.BlockSpec(memory_space=pltpu.SMEM)
     leave = pl.BlockSpec(memory_space=pl.ANY)
     arrays = [part for block in token_parts for part in block] + [w_blocks] + list(kv_parts)
-    counts = (parts, len(kv_parts), mask_width)
+    counts = (parts, len(kv_parts), halves, mask_width)
     tile_rows = heads * QUERIES
 
     def kernel(*refs):
@@ -290,12 +291,11 @@
     first_columns = (q_width // HD + 1) // 2 * HD
     cuts = ((0, first_columns), (first_columns, q_width))
 
-    marks_own = marks_of(doc_start, tile_mask)
+    kv_own = jnp.stack([cache_keys, cache_values])
     w_first = [columns_for(w_query, d, cuts[0][0], cuts[0][1] - cuts[0][0], q_width, 1) for d in range(group)]
-    kv_own = after([cache_keys, cache_values], *w_first)
+    w_first = after(w_first, kv_own)
     w_first = w_first[:1] + [swapped(w_first[d], d) for d in far]
-    hop = [(i, i + group) for i in range(devices - group)]
-    kv_before = [lax.ppermute(array, "ctx", hop) for array in kv_own]
+    kv_before = lax.ppermute(kv_own, "ctx", [(i, i + group) for i in range(devices - group)])
 
     float_tokens = tokens.astype(jnp.float32)
     squares = jnp.sum(float_tokens * float_tokens, axis=-1)
@@ -307,20 +307,23 @@
     w_second = [columns_for(w_query, d, cuts[1][0], cuts[1][1] - cuts[1][0], q_width, 1) for d in range(group)]
     w_second = after(w_second, *w_first)
     w_second = w_second[:1] + [swapped(w_second[d], d) for d in far]
-    w_stack = jnp.stack(after(w_first, *kv_before))
+    w_stack = jnp.stack(after(w_first, kv_before))
     w_chunks = [lax.all_gather(w_stack, "ctx", axis=0, tiled=True, axis_index_groups=lines)]
-    (marks_sent,) = after([marks_own], w_stack)
-    marks = [marks_own] + [swapped(marks_sent, d) for d in far]
+
+    marks_own = marks_of(doc_start, tile_mask)
+    marks_rows = marks_own.shape[0]
+    bytes_own = jnp.concatenate([marks_own >> 16, (marks_own >> 8) & 255, marks_own & 255]).astype(jnp.bfloat16)
+    bytes_own = jnp.pad(bytes_own, ((0, -bytes_own.shape[0] % 16), (0, 0)))
 
     def kv_for(d):
-        arrays = (*kv_before, cache_keys, cache_values)
-        return jnp.stack([columns_for(array, d, 0, kv_width, kv_width, 1) for array in arrays]).reshape(
-            2, 2, tok_rows, kv_width
-        )
-
-    kv_cut = [kv_for(d) for d in range(group)]
-    kv_parts = kv_cut[:1] + [swapped(kv_cut[d], d) for d in far]
-    (normed,) = after([normed], *marks, *kv_cut, *w_second)
+        cut = [columns_for(array, d, 0, kv_width, kv_width, 2).reshape(-1, kv_width) for array in (kv_before, kv_own)]
+        return jnp.concatenate(cut + [bytes_own])
+
+    kv_parts = [kv_for(0)] + [swapped(kv_for(d), d) for d in far]
+
+    sent = jnp.stack([part[4 * tok_rows :] for part in kv_parts]).astype(jnp.int32)
+    marks = sent[:, :marks_rows] * 65536 + sent[:, marks_rows : 2 * marks_rows] * 256
+    marks = marks + sent[:, 2 * marks_rows : 3 * marks_rows]
     from_x, from_y = swapped(normed, 1), swapped(normed, 2)
     mine_other = other_core(normed)
     (w_after,) = after([jnp.stack(w_second)], *kv_parts)
@@ -337,8 +340,7 @@
     def call(distances, chunk, *earlier):
         chosen = [token_parts[d] for d in distances]
         (start,) = after([info], *earlier)
-        picked = jnp.stack([marks[d] for d in distances])
-        return attend(start, picked, distances, chosen, chunk, kv_parts, width_mask)
+        return attend(start, marks, distances, chosen, chunk, kv_parts, 2, width_mask)
 
     pieces, last = {}, ()
     for chunk, distances in ((0, (2, 1, 0)), (0, (3,)), (1, (3, 2, 1)), (1, (0,))):
@@ -397,7 +399,8 @@
             (0,),
             [[normed]],
             w_blocks[:, :, head * q_width : (head + 1) * q_width],
-            [kv_window[:, :, :, head * HD : (head + 1) * HD]],
+            [kv_window[:, :, :, head * HD : (head + 1) * HD].reshape(-1, HD)],
+            reach + 1,
             tile_mask.shape[1],
         )[0]
         for head in range(kv_heads)

time: 253 us -> 250 us (0.988)
  other arithmetic: 19.2 us -> 11 us
  Pallas kernels: 75.1 us -> 80.5 us
  waiting for transfers between devices: 91.7 us -> 94.5 us
    ppermute x22 -> x19, waiting for transfers between devices: 81.3 us -> 87.1 us  [swapped(): lax.ppermute(block, 'ctx', [(i, i ^ distance) for i in range(devices)])]
    pallas_call x4, Pallas kernels: 71.7 us -> 77.1 us  [attend(): pl.pallas_call(kernel, out_shape=[jax.ShapeDtypeStruct((rows, columns), j...]
    another operation x6 -> x5, other arithmetic: 9.51 us -> 4.76 us  [the longest x2 3.59 us: planar(): kv_own = jnp.stack([cache_keys, cache_values])]
    all_gather x1, waiting for transfers between devices: 3.42 us -> 0.02 us  [planar(): lax.all_gather(w_after, 'ctx', axis=0, tiled=True, axis_index_groups=lines)]
    ppermute x22 -> x19, starting transfers between devices: 25.6 us -> 27.2 us  [swapped(): lax.ppermute(block, 'ctx', [(i, i ^ distance) for i in range(devices)])]
    ppermute x2 -> x1, starting transfers between devices: 7.73 us -> 6.19 us  [planar(): lax.ppermute(kv_own, 'ctx', [(i, i + group) for i in range(devices - grou...]
    ppermute x2 -> x1, waiting for transfers between devices: 5.68 us -> 6.33 us  [planar(): lax.ppermute(kv_own, 'ctx', [(i, i + group) for i in range(devices - grou...]
  transfers between devices with their start and end apart: 31 -> 27, of which waited for: 10 -> 9; matrix products, arithmetic and copies ran while one was open for 13% -> 8% of each run, Pallas kernels for 29% -> 31%
where the time goes in v2:
time: 250 us
  waiting for transfers between devices  94.5 us (38%)
  Pallas kernels  80.5 us (32%)
  starting transfers between devices  34.1 us (14%)
  local copies, waits for them, and re-layouts  15.7 us (6%)
  between operations  13.8 us (6%)
  other arithmetic  11 us (4%)
    ppermute x19, waiting for transfers between devices, swapped(): lax.ppermute(block, 'ctx', [(i, i ^ distance) for i in range(devices)])  87.1 us
    pallas_call x4, Pallas kernels, attend(): pl.pallas_call(kernel, out_shape=[jax.ShapeDtypeStruct((rows, columns), j...  77.1 us
    ppermute x19, starting transfers between devices, swapped(): lax.ppermute(block, 'ctx', [(i, i ^ distance) for i in range(devices)])  27.2 us
    ppermute x1, waiting for transfers between devices, planar(): lax.ppermute(kv_own, 'ctx', [(i, i + group) for i in range(devices - grou...  6.33 us
    ppermute x1, starting transfers between devices, planar(): lax.ppermute(kv_own, 'ctx', [(i, i + group) for i in range(devices - grou...  6.19 us
  transfers between devices with their start and end apart: 27, of which 9 were waited for; matrix products, arithmetic and copies ran while one was open for 8% of the time, Pallas kernels for 31%

profile of v2, /device:TPU:0, one launch (start us, length us, event | category | flops | bytes accessed | tf_op | source)
XLA Modules:
  0.0 249.6 jit_solution(7590926184391078232)
XLA Ops:
  6.5 2.3 pad_maximum_fusion
  8.8 6.2 %collective-permute-start = (bf16[2,512,512]{2,1,0:T(8,128)(2,1)}, bf16[2,512,512]{2,1,0:T(8,128)(2,1)}, u32[]{:S(2)}, u32[]{:S(2)}) collective-permute-start(bf16[2,512,512]{2,1,0:T(8,128)(2,1)} %pad_maximum_fusion), channel_id=1, source_target_pairs={{0,8},{2,10},{4,12},{6,14},{8,16},{10,18},{12,20},{14,22},{16,24},... | collective-permute-start | bytes 3145736 | tf_op jit(solution)/shard_map/ppermute | solution.py:298
  16.4 1.6 collective-permute-start.7
  18.0 1.5 collective-permute-start.8
  20.0 5.4 %collective-permute-done.7 = bf16[320,384]{1,0:T(8,128)(2,1)S(1)} collective-permute-done((bf16[320,384]{1,0:T(8,128)(2,1)S(1)}, bf16[320,384]{1,0:T(8,128)(2,1)S(1)}, u32[]{:S(2)}, u32[]{:S(2)}) %collective-permute-start.7) | collective-permute-done | bytes 245792 | tf_op jit(solution)/shard_map/ppermute | solution.py:278
  25.4 5.0 %collective-permute-done.8 = bf16[320,384]{1,0:T(8,128)(2,1)S(1)} collective-permute-done((bf16[320,384]{1,0:T(8,128)(2,1)S(1)}, bf16[320,384]{1,0:T(8,128)(2,1)S(1)}, u32[]{:S(2)}, u32[]{:S(2)}) %collective-permute-start.8) | collective-permute-done | bytes 245792 | tf_op jit(solution)/shard_map/ppermute | solution.py:278
  30.4 6.3 %collective-permute-done = bf16[2,512,512]{2,1,0:T(8,128)(2,1)} collective-permute-done((bf16[2,512,512]{2,1,0:T(8,128)(2,1)}, bf16[2,512,512]{2,1,0:T(8,128)(2,1)}, u32[]{:S(2)}, u32[]{:S(2)}) %collective-permute-start) | collective-permute-done | bytes 1048608 | tf_op jit(solution)/shard_map/ppermute | solution.py:298
  39.8 2.2 fusion.2.refs_7_.refs_3_
  41.9 1.5 collective-permute-start.5
  43.4 1.5 collective-permute-start.6
  48.7 2.5 %collective-permute-start.12 = (bf16[320,256]{1,0:T(8,128)(2,1)S(1)}, bf16[320,256]{1,0:T(8,128)(2,1)S(1)}, u32[]{:S(2)}, u32[]{:S(2)}) collective-permute-start(bf16[320,256]{1,0:T(8,128)(2,1)S(1)} %get-tuple-element.38), channel_id=1, source_target_pairs={{0,6},{2,4},{4,2},{6,0},{8,14},{10,12},{12,10},{14,8},{16,22},{18,... | collective-permute-start | bytes 491528 | tf_op jit(solution)/shard_map/ppermute | solution.py:278
  53.7 51.6 %collective-permute-done.10 = bf16[320,256]{1,0:T(8,128)(2,1)S(1)} collective-permute-done((bf16[320,256]{1,0:T(8,128)(2,1)S(1)}, bf16[320,256]{1,0:T(8,128)(2,1)S(1)}, u32[]{:S(2)}, u32[]{:S(2)}) %collective-permute-start.10) | collective-permute-done | bytes 163872 | tf_op jit(solution)/shard_map/ppermute | solution.py:278
  105.4 1.5 collective-permute-start.1
  106.9 1.9 collective-permute-done.11
  108.8 2.1 collective-permute-start.2
  112.2 8.2 %collective-permute-done.1.refs_11_.refs_7_ = bf16[2080,128]{1,0:T(8,128)(2,1)S(1)} collective-permute-done((bf16[2080,128]{1,0:T(8,128)(2,1)S(1)}, bf16[2080,128]{1,0:T(8,128)(2,1)S(1)}, u32[]{:S(2)}, u32[]{:S(2)}) %collective-permute-start.1) | collective-permute-done | bytes 532512 | tf_op jit(solution)/shard_map/ppermute | solution.py:278
  120.4 12.9 %collective-permute-done.2.refs_12_.refs_8_ = bf16[2080,128]{1,0:T(8,128)(2,1)} collective-permute-done((bf16[2080,128]{1,0:T(8,128)(2,1)}, bf16[2080,128]{1,0:T(8,128)(2,1)}, u32[]{:S(2)}, u32[]{:S(2)}) %collective-permute-start.2) | collective-permute-done | bytes 532512 | tf_op jit(solution)/shard_map/ppermute | solution.py:278
  135.3 2.5 slice.30
  137.8 2.5 slice.31
  140.3 1.7 collective-permute-start.17
  143.4 1.4 copy-done.2
  144.8 28.1 %shard_map.73 = (bf16[512,384]{1,0:T(8,128)(2,1)}, bf16[512,384]{1,0:T(8,128)(2,1)}, bf16[512,384]{1,0:T(8,128)(2,1)}) custom-call(s32[3]{0:T(128)} %pad_add_fusion.1.refs_0_.info_ref, s32[4,6,128]{2,1,0:T(8,128)} %fusion.8.refs_1_.refs_2_, s32[4,6,128]{2,1,0:T(8,128)} %fusion.8.refs_1_.refs_2_, bf16[512,2560]{1,0:T(8,128)(2,1)} %collective-permute-done.6.refs_3_.refs_5_, ...), custom_call_target="tpu_custom_call" | custom-call | flops 8455716864 | bytes 22937600 | tf_op jit(solution)/shard_map/pallas_call | solution.py:230
  172.9 1.5 constant_dynamic-update-slice_fusion.1
  174.4 1.4 constant_dynamic-update-slice_fusion.refs_3_
  175.9 4.1 %collective-permute-start.21 = (bf16[512,384]{1,0:T(8,128)(2,1)S(1)}, bf16[512,384]{1,0:T(8,128)(2,1)S(1)}, u32[]{:S(2)}, u32[]{:S(2)}) collective-permute-start(bf16[512,384]{1,0:T(8,128)(2,1)S(1)} %copy-done.14), channel_id=1, source_target_pairs={{0,4},{2,6},{4,0},{6,2},{8,12},{10,14},{12,8},{14,10},{16,20},{18,... | collective-permute-start | bytes 1179656 | tf_op jit(solution)/shard_map/ppermute | solution.py:278
  180.0 3.6 %collective-permute-start.19 = (bf16[512,384]{1,0:T(8,128)(2,1)}, bf16[512,384]{1,0:T(8,128)(2,1)S(1)}, u32[]{:S(2)}, u32[]{:S(2)}) collective-permute-start(bf16[512,384]{1,0:T(8,128)(2,1)} %get-tuple-element.54), channel_id=1, source_target_pairs={{0,2},{2,0},{4,6},{6,4},{8,10},{10,8},{12,14},{14,12},{16,18},{18,... | collective-permute-start | bytes 1179656 | tf_op jit(solution)/shard_map/ppermute | solution.py:278
  183.6 16.1 %shard_map.74 = bf16[512,384]{1,0:T(8,128)(2,1)} custom-call(s32[3]{0:T(128)} %pad_add_fusion.1.refs_0_.info_ref, s32[4,6,128]{2,1,0:T(8,128)} %fusion.8.refs_1_.refs_2_, s32[4,6,128]{2,1,0:T(8,128)} %fusion.8.refs_1_.refs_2_, bf16[512,2560]{1,0:T(8,128)(2,1)} %copy-done.1, bf16[512,2560]{1,0:T(8,128)(2,1)} %collective-permute-done.18.refs_4_, ...), custom_call_target="tpu_custom_call" | custom-call | flops 2818572288 | bytes 11665408 | tf_op jit(solution)/shard_map/pallas_call | solution.py:230
  199.8 24.5 %shard_map.75 = (bf16[512,256]{1,0:T(8,128)(2,1)}, bf16[512,256]{1,0:T(8,128)(2,1)}, bf16[512,256]{1,0:T(8,128)(2,1)}) custom-call(s32[3]{0:T(128)} %pad_add_fusion.1.refs_0_.info_ref, s32[4,6,128]{2,1,0:T(8,128)} %fusion.8.refs_1_.refs_2_, s32[4,6,128]{2,1,0:T(8,128)} %fusion.8.refs_1_.refs_2_, bf16[512,2560]{1,0:T(8,128)(2,1)} %copy-done.1, ...), custom_call_target="tpu_custom_call" | custom-call | flops 5637144576 | bytes 21233664 | tf_op jit(solution)/shard_map/pallas_call | solution.py:230
  224.5 3.4 %collective-permute-start.24 = (bf16[512,256]{1,0:T(8,128)(2,1)}, bf16[512,256]{1,0:T(8,128)(2,1)S(1)}, u32[]{:S(2)}, u32[]{:S(2)}) collective-permute-start(bf16[512,256]{1,0:T(8,128)(2,1)} %get-tuple-element.52), channel_id=1, source_target_pairs={{0,6},{2,4},{4,2},{6,0},{8,14},{10,12},{12,10},{14,8},{16,22},{18,... | collective-permute-start | bytes 786440 | tf_op jit(solution)/shard_map/ppermute | solution.py:278
  227.9 8.4 %shard_map.76.refs_1_ = bf16[512,256]{1,0:T(8,128)(2,1)} custom-call(s32[3]{0:T(128)} %pad_add_fusion.1.refs_0_.info_ref, s32[4,6,128]{2,1,0:T(8,128)} %fusion.8.refs_1_.refs_2_, s32[4,6,128]{2,1,0:T(8,128)} %fusion.8.refs_1_.refs_2_, bf16[512,2560]{1,0:T(8,128)(2,1)} %fusion.2.refs_7_.refs_3_, bf16[512,2560]{1,0:T(8,128)(2,1)} %copy-done.2, ...), custom_call_target="tpu_custom_call" | custom-call | flops 1879048192 | bytes 10223616 | tf_op jit(solution)/shard_map/pallas_call | solution.py:230
  236.4 2.0 collective-permute-done.22.refs_5_
  239.3 3.4 %shard_map.77 = bf16[512,2560]{1,0:T(8,128)(2,1)} custom-call(s32[3]{0:T(128)} %pad_add_fusion.1.refs_0_.info_ref, bf16[512,384]{1,0:T(8,128)(2,1)} %get-tuple-element.46.refs_0_, bf16[512,256]{1,0:T(8,128)(2,1)} %shard_map.76.refs_1_, bf16[512,384]{1,0:T(8,128)(2,1)} %copy-done.6, bf16[512,256]{1,0:T(8,128)(2,1)} %copy-done.8, bf16[512,384]{1,0:T(8,128)(2,1)} %copy-done.5, ...), custom_call_target="tpu_custom_call" | custom-call | bytes 5242880 | tf_op jit(solution)/shard_map/pallas_call | solution.py:367
  (84 shorter events, 17.2 us)
Async XLA Ops:
  6.5 136.8 %all-gather.3.cloned.1.call-start = ((), (), s32[]{:S(2)}) async-start(), calls=%async_computation | async-start | bytes 4915200 | tf_op jit(solution)/shard_map/all_gather | solution.py:311
  8.8 29.1 %copy-start = (bf16[512,2560]{1,0:T(8,128)(2,1)S(1)}, bf16[512,2560]{1,0:T(8,128)(2,1)}, u32[]{:S(2)}) copy-start(bf16[512,2560]{1,0:T(8,128)(2,1)} %param.7) | copy-start | bytes 7864324
  8.8 27.9 %collective-permute-start = (bf16[2,512,512]{2,1,0:T(8,128)(2,1)}, bf16[2,512,512]{2,1,0:T(8,128)(2,1)}, u32[]{:S(2)}, u32[]{:S(2)}) collective-permute-start(bf16[2,512,512]{2,1,0:T(8,128)(2,1)} %pad_maximum_fusion), channel_id=1, source_target_pairs={{0,8},{2,10},{4,12},{6,14},{8,16},{10,18},{12,20},{14,22},{16,24},... | collective-permute-start | bytes 3145736 | tf_op jit(solution)/shard_map/ppermute | solution.py:298
  16.4 8.9 %collective-permute-start.7 = (bf16[320,384]{1,0:T(8,128)(2,1)S(1)}, bf16[320,384]{1,0:T(8,128)(2,1)S(1)}, u32[]{:S(2)}, u32[]{:S(2)}) collective-permute-start(bf16[320,384]{1,0:T(8,128)(2,1)S(1)} %get-tuple-element.32), channel_id=1, source_target_pairs={{0,2},{2,0},{4,6},{6,4},{8,10},{10,8},{12,14},{14,12},{16,18},{18,... | collective-permute-start | bytes 737288 | tf_op jit(solution)/shard_map/ppermute | solution.py:278
  18.0 12.4 %collective-permute-start.8 = (bf16[320,384]{1,0:T(8,128)(2,1)S(1)}, bf16[320,384]{1,0:T(8,128)(2,1)S(1)}, u32[]{:S(2)}, u32[]{:S(2)}) collective-permute-start(bf16[320,384]{1,0:T(8,128)(2,1)S(1)} %get-tuple-element.33), channel_id=1, source_target_pairs={{0,4},{2,6},{4,0},{6,2},{8,12},{10,14},{12,8},{14,10},{16,20},{18,... | collective-permute-start | bytes 737288 | tf_op jit(solution)/shard_map/ppermute | solution.py:278
  19.5 10.9 %collective-permute-start.9 = (bf16[320,384]{1,0:T(8,128)(2,1)S(1)}, bf16[320,384]{1,0:T(8,128)(2,1)S(1)}, u32[]{:S(2)}, u32[]{:S(2)}) collective-permute-start(bf16[320,384]{1,0:T(8,128)(2,1)S(1)} %get-tuple-element.34), channel_id=1, source_target_pairs={{0,6},{2,4},{4,2},{6,0},{8,14},{10,12},{12,10},{14,8},{16,22},{18,... | collective-permute-start | bytes 737288 | tf_op jit(solution)/shard_map/ppermute | solution.py:278
  37.9 161.9 %all-gather.5.cloned.1.call-start = ((), (), s32[]{:S(2)}) async-start(), calls=%async_computation.1 | async-start | bytes 3276800 | tf_op jit(solution)/shard_map/all_gather | solution.py:330
  38.5 1.2 collective-permute-start.4
  39.8 6.5 %copy-start.4 = (bf16[512,512]{1,0:T(8,128)(2,1)S(1)}, bf16[512,512]{1,0:T(8,128)(2,1)}, u32[]{:S(2)}) copy-start(bf16[512,512]{1,0:T(8,128)(2,1)} %param.10) | copy-start | bytes 1572868
  41.9 91.4 %collective-permute-start.5 = (bf16[512,2560]{1,0:T(8,128)(2,1)}, bf16[512,2560]{1,0:T(8,128)(2,1)}, u32[]{:S(2)}, u32[]{:S(2)}) collective-permute-start(bf16[512,2560]{1,0:T(8,128)(2,1)} %fusion.2.refs_7_.refs_3_), channel_id=1, source_target_pairs={{0,2},{2,0},{4,6},{6,4},{8,10},{10,8},{12,14},{14,12},{16,18},{18,... | collective-permute-start | bytes 7864328 | tf_op jit(solution)/shard_map/ppermute | solution.py:278
  43.4 89.9 %collective-permute-start.6 = (bf16[512,2560]{1,0:T(8,128)(2,1)}, bf16[512,2560]{1,0:T(8,128)(2,1)}, u32[]{:S(2)}, u32[]{:S(2)}) collective-permute-start(bf16[512,2560]{1,0:T(8,128)(2,1)} %fusion.2.refs_7_.refs_3_), channel_id=1, source_target_pairs={{0,4},{2,6},{4,0},{6,2},{8,12},{10,14},{12,8},{14,10},{16,20},{18,... | collective-permute-start | bytes 7864328 | tf_op jit(solution)/shard_map/ppermute | solution.py:278
  47.6 57.7 %collective-permute-start.10 = (bf16[320,256]{1,0:T(8,128)(2,1)S(1)}, bf16[320,256]{1,0:T(8,128)(2,1)S(1)}, u32[]{:S(2)}, u32[]{:S(2)}) collective-permute-start(bf16[320,256]{1,0:T(8,128)(2,1)S(1)} %get-tuple-element.36), channel_id=1, source_target_pairs={{0,2},{2,0},{4,6},{6,4},{8,10},{10,8},{12,14},{14,12},{16,18},{18,... | collective-permute-start | bytes 491528 | tf_op jit(solution)/shard_map/ppermute | solution.py:278
  48.1 60.6 %collective-permute-start.11 = (bf16[320,256]{1,0:T(8,128)(2,1)S(1)}, bf16[320,256]{1,0:T(8,128)(2,1)S(1)}, u32[]{:S(2)}, u32[]{:S(2)}) collective-permute-start(bf16[320,256]{1,0:T(8,128)(2,1)S(1)} %get-tuple-element.37), channel_id=1, source_target_pairs={{0,4},{2,6},{4,0},{6,2},{8,12},{10,14},{12,8},{14,10},{16,20},{18,... | collective-permute-start | bytes 491528 | tf_op jit(solution)/shard_map/ppermute | solution.py:278
  48.7 62.2 %collective-permute-start.12 = (bf16[320,256]{1,0:T(8,128)(2,1)S(1)}, bf16[320,256]{1,0:T(8,128)(2,1)S(1)}, u32[]{:S(2)}, u32[]{:S(2)}) collective-permute-start(bf16[320,256]{1,0:T(8,128)(2,1)S(1)} %get-tuple-element.38), channel_id=1, source_target_pairs={{0,6},{2,4},{4,2},{6,0},{8,14},{10,12},{12,10},{14,8},{16,22},{18,... | collective-permute-start | bytes 491528 | tf_op jit(solution)/shard_map/ppermute | solution.py:278
  105.4 15.0 %collective-permute-start.1 = (bf16[2080,128]{1,0:T(8,128)(2,1)S(1)}, bf16[2080,128]{1,0:T(8,128)(2,1)S(1)}, u32[]{:S(2)}, u32[]{:S(2)}) collective-permute-start(bf16[2080,128]{1,0:T(8,128)(2,1)S(1)} %get-tuple-element.76), channel_id=1, source_target_pairs={{0,2},{2,0},{4,6},{6,4},{8,10},{10,8},{12,14},{14,12},{16,18},{18,... | collective-permute-start | bytes 1597448 | tf_op jit(solution)/shard_map/ppermute | solution.py:278
  108.8 24.6 %collective-permute-start.2 = (bf16[2080,128]{1,0:T(8,128)(2,1)}, bf16[2080,128]{1,0:T(8,128)(2,1)}, u32[]{:S(2)}, u32[]{:S(2)}) collective-permute-start(bf16[2080,128]{1,0:T(8,128)(2,1)} %get-tuple-element.74), channel_id=1, source_target_pairs={{0,4},{2,6},{4,0},{6,2},{8,12},{10,14},{12,8},{14,10},{16,20},{18,... | collective-permute-start | bytes 1597448 | tf_op jit(solution)/shard_map/ppermute | solution.py:278
  110.8 22.5 %collective-permute-start.3 = (bf16[2080,128]{1,0:T(8,128)(2,1)}, bf16[2080,128]{1,0:T(8,128)(2,1)}, u32[]{:S(2)}, u32[]{:S(2)}) collective-permute-start(bf16[2080,128]{1,0:T(8,128)(2,1)} %get-tuple-element.75), channel_id=1, source_target_pairs={{0,6},{2,4},{4,2},{6,0},{8,14},{10,12},{12,10},{14,8},{16,22},{18,... | collective-permute-start | bytes 1597448 | tf_op jit(solution)/shard_map/ppermute | solution.py:278
  120.4 22.3 %copy-start.3 = (bf16[2080,128]{1,0:T(8,128)(2,1)}, bf16[2080,128]{1,0:T(8,128)(2,1)S(1)}, u32[]{:S(2)}) copy-start(bf16[2080,128]{1,0:T(8,128)(2,1)S(1)} %collective-permute-done.1.refs_11_.refs_7_) | copy-start | bytes 1597444
  120.4 22.9 %collective-permute-start.15 = (bf16[512,2560]{1,0:T(8,128)(2,1)}, bf16[512,2560]{1,0:T(8,128)(2,1)S(1)}, u32[]{:S(2)}, u32[]{:S(2)}) collective-permute-start(bf16[512,2560]{1,0:T(8,128)(2,1)} %fusion.2.refs_7_.refs_3_), channel_id=1, source_target_pairs={{0,1},{1,0},{2,3},{3,2},{4,5},{5,4},{6,7},{7,6},{8,9},{9,8},{10,11... | collective-permute-start | bytes 7864328 | tf_op jit(solution)/shard_map/ppermute | solution.py:281
  133.3 10.0 %collective-permute-start.13 = (bf16[512,2560]{1,0:T(8,128)(2,1)}, bf16[512,2560]{1,0:T(8,128)(2,1)}, u32[]{:S(2)}, u32[]{:S(2)}) collective-permute-start(bf16[512,2560]{1,0:T(8,128)(2,1)} %collective-permute-done.6.refs_3_.refs_5_), channel_id=1, source_target_pairs={{0,1},{1,0},{2,3},{3,2},{4,5},{5,4},{6,7},{7,6},{8,9},{9,8},{10,11... | collective-permute-start | bytes 7864328 | tf_op jit(solution)/shard_map/ppermute | solution.py:281
  133.4 9.9 %collective-permute-start.14 = (bf16[512,2560]{1,0:T(8,128)(2,1)}, bf16[512,2560]{1,0:T(8,128)(2,1)}, u32[]{:S(2)}, u32[]{:S(2)}) collective-permute-start(bf16[512,2560]{1,0:T(8,128)(2,1)} %collective-permute-done.5.refs_5_.refs_7_), channel_id=1, source_target_pairs={{0,1},{1,0},{2,3},{3,2},{4,5},{5,4},{6,7},{7,6},{8,9},{9,8},{10,11... | collective-permute-start | bytes 7864328 | tf_op jit(solution)/shard_map/ppermute | solution.py:281
  140.3 32.6 %collective-permute-start.16 = (bf16[512,1280]{1,0:T(8,128)(2,1)}, bf16[512,1280]{1,0:T(8,128)(2,1)}, u32[]{:S(2)}, u32[]{:S(2)}) collective-permute-start(bf16[512,1280]{1,0:T(8,128)(2,1)} %slice.30), channel_id=1, source_target_pairs={{0,2},{2,0},{4,6},{6,4},{8,10},{10,8},{12,14},{14,12},{16,18},{18,... | collective-permute-start | bytes 3932168 | tf_op jit(solution)/shard_map/ppermute | solution.py:278
  140.3 32.5 %collective-permute-start.17 = (bf16[512,1280]{1,0:T(8,128)(2,1)}, bf16[512,1280]{1,0:T(8,128)(2,1)}, u32[]{:S(2)}, u32[]{:S(2)}) collective-permute-start(bf16[512,1280]{1,0:T(8,128)(2,1)} %slice.31), channel_id=1, source_target_pairs={{0,4},{2,6},{4,0},{6,2},{8,12},{10,14},{12,8},{14,10},{16,20},{18,... | collective-permute-start | bytes 3932168 | tf_op jit(solution)/shard_map/ppermute | solution.py:278
  175.8 7.8 %copy-start.1 = (bf16[512,2560]{1,0:T(8,128)(2,1)}, bf16[512,2560]{1,0:T(8,128)(2,1)S(1)}, u32[]{:S(2)}) copy-start(bf16[512,2560]{1,0:T(8,128)(2,1)S(1)} %constant_dynamic-update-slice_fusion.refs_3_) | copy-start | bytes 7864324
  175.8 7.8 %collective-permute-start.18 = (bf16[512,2560]{1,0:T(8,128)(2,1)S(1)}, bf16[512,2560]{1,0:T(8,128)(2,1)}, u32[]{:S(2)}, u32[]{:S(2)}) collective-permute-start(bf16[512,2560]{1,0:T(8,128)(2,1)S(1)} %constant_dynamic-update-slice_fusion.refs_3_), channel_id=1, source_target_pairs={{0,1},{1,0},{2,3},{3,2},{4,5},{5,4},{6,7},{7,6},{8,9},{9,8},{10,11... | collective-permute-start | bytes 7864328 | tf_op jit(solution)/shard_map/ppermute | solution.py:281
  175.9 60.4 %collective-permute-start.21 = (bf16[512,384]{1,0:T(8,128)(2,1)S(1)}, bf16[512,384]{1,0:T(8,128)(2,1)S(1)}, u32[]{:S(2)}, u32[]{:S(2)}) collective-permute-start(bf16[512,384]{1,0:T(8,128)(2,1)S(1)} %copy-done.14), channel_id=1, source_target_pairs={{0,4},{2,6},{4,0},{6,2},{8,12},{10,14},{12,8},{14,10},{16,20},{18,... | collective-permute-start | bytes 1179656 | tf_op jit(solution)/shard_map/ppermute | solution.py:278
  180.0 44.5 %collective-permute-start.19 = (bf16[512,384]{1,0:T(8,128)(2,1)}, bf16[512,384]{1,0:T(8,128)(2,1)S(1)}, u32[]{:S(2)}, u32[]{:S(2)}) collective-permute-start(bf16[512,384]{1,0:T(8,128)(2,1)} %get-tuple-element.54), channel_id=1, source_target_pairs={{0,2},{2,0},{4,6},{6,4},{8,10},{10,8},{12,14},{14,12},{16,18},{18,... | collective-permute-start | bytes 1179656 | tf_op jit(solution)/shard_map/ppermute | solution.py:278
  199.7 38.7 %collective-permute-start.23 = (bf16[512,384]{1,0:T(8,128)(2,1)}, bf16[512,384]{1,0:T(8,128)(2,1)S(1)}, u32[]{:S(2)}, u32[]{:S(2)}) collective-permute-start(bf16[512,384]{1,0:T(8,128)(2,1)} %shard_map.74), channel_id=1, source_target_pairs={{0,6},{2,4},{4,2},{6,0},{8,14},{10,12},{12,10},{14,8},{16,22},{18,... | collective-permute-start | bytes 1179656 | tf_op jit(solution)/shard_map/ppermute | solution.py:278
  224.3 12.0 %collective-permute-start.20 = (bf16[512,256]{1,0:T(8,128)(2,1)}, bf16[512,256]{1,0:T(8,128)(2,1)S(1)}, u32[]{:S(2)}, u32[]{:S(2)}) collective-permute-start(bf16[512,256]{1,0:T(8,128)(2,1)} %get-tuple-element.55), channel_id=1, source_target_pairs={{0,2},{2,0},{4,6},{6,4},{8,10},{10,8},{12,14},{14,12},{16,18},{18,... | collective-permute-start | bytes 786440 | tf_op jit(solution)/shard_map/ppermute | solution.py:278
  224.4 14.0 %collective-permute-start.22 = (bf16[512,256]{1,0:T(8,128)(2,1)}, bf16[512,256]{1,0:T(8,128)(2,1)S(1)}, u32[]{:S(2)}, u32[]{:S(2)}) collective-permute-start(bf16[512,256]{1,0:T(8,128)(2,1)} %get-tuple-element.56), channel_id=1, source_target_pairs={{0,4},{2,6},{4,0},{6,2},{8,12},{10,14},{12,8},{14,10},{16,20},{18,... | collective-permute-start | bytes 786440 | tf_op jit(solution)/shard_map/ppermute | solution.py:278
  224.5 11.8 %copy-start.6 = (bf16[512,384]{1,0:T(8,128)(2,1)}, bf16[512,384]{1,0:T(8,128)(2,1)S(1)}, u32[]{:S(2)}) copy-start(bf16[512,384]{1,0:T(8,128)(2,1)S(1)} %collective-permute-done.19.refs_2_) | copy-start | bytes 1179652
  224.5 13.9 %collective-permute-start.24 = (bf16[512,256]{1,0:T(8,128)(2,1)}, bf16[512,256]{1,0:T(8,128)(2,1)S(1)}, u32[]{:S(2)}, u32[]{:S(2)}) collective-permute-start(bf16[512,256]{1,0:T(8,128)(2,1)} %get-tuple-element.52), channel_id=1, source_target_pairs={{0,6},{2,4},{4,2},{6,0},{8,14},{10,12},{12,10},{14,8},{16,22},{18,... | collective-permute-start | bytes 786440 | tf_op jit(solution)/shard_map/ppermute | solution.py:278
  (10 other events, 23.4 us)
Sparse Core Ops, SparseCore 0:
  38.0 78.5 all-gather.2
  134.7 56.2 all-gather.4
